TPU v7x, 256 devices: a whole 4x4x8 slice. The times are simulated.
256 devices in a mesh: dp: 32 (over y, x, core), ind: 8 (over z).
Axes of the slice: x: 4, y: 4, z: 8, core: 2. Of those that a mesh axis runs over, the one named last changes fastest.
Arguments:
- inputs: bfloat16 [65536, 256], P('dp'), may hold values from -6 to 6
- targets: bfloat16 [65536], P('dp'), may hold values from -6 to 6
- row_counts: int32 [32], replicated, may hold values from 1 to 2048, 32768 in all
- w_in: bfloat16 [256, 1024], replicated, may hold values from -0.375 to 0.375
- w_mid: bfloat16 [1024, 1024], replicated, may hold values from -0.1875 to 0.1875
- w_out: bfloat16 [1024, 128], replicated, may hold values from -0.1875 to 0.1875
- feat_gain: float32 [128], replicated, may hold values from 0.1 to 1.9
- inducing: bfloat16 [16384, 128], P('ind'), may hold values from -6 to 6
- log_scale: float32 [1], replicated, may hold values from -0.5 to 0.5
- lengthscale: float32 [1], replicated, may hold values from 3.2 to 3.5
- noise_var: float32 [1], replicated, may hold values from 5e-05 to 0.0002
Outputs:
- panel_factor: float32 [16384, 512], P(('ind', 'dp'))
- rhs_next: float32 [16384], P(('ind', 'dp'))
- panel_solution: float32 [512], replicated
- log_det: float32 [1], replicated
Inputs may be any that keep to these rules, and one draw needn't show every extreme that they name: The first row_counts[s] samples of shard s are valid; the counts sum to 32768 and one shard has all 2048 slots valid.
All inputs are finite; a program needn't handle non-finite values.
Results may differ from a plain program's by a relative error of at most 0.012.
The roundings to bfloat16 on the way count: a program that leaves them out, or rounds other values in their place, can miss the bound.
Values may be sent and summed in bfloat16 or wider, within the bound.
No kernel may reach another device: no remote copies, remote signals or barrier semaphores. Data moves between devices by JAX's collectives and lax.ppermute only.
A program may use at most 64 MiB of HBM per device.

v0:
```python
import functools
import jax
import jax.numpy as jnp
from jax import lax
from jax.experimental import pallas as pl
from jax.experimental.pallas import tpu as pltpu
from jax.sharding import PartitionSpec as P


PB = 512
JITTER = 0.0001
SHARDS, LAYERS = 32, 8
LOG2E = 1.4426950408889634
MASKED = -1.0e6
F32, BF16 = jnp.float32, jnp.bfloat16
HI = lax.Precision.HIGHEST
NT = (((1,), (1,)), ((), ()))
TN = (((0,), (0,)), ((), ()))


def vmem(limit=60 << 20):
    return pltpu.CompilerParams(vmem_limit_bytes=limit)


def widen(points, half, first):
    rows = points.shape[0]
    high = half.astype(BF16)
    rest = half - high.astype(F32)
    mid = rest.astype(BF16)
    low = (rest - mid.astype(F32)).astype(BF16)
    lane = lax.broadcasted_iota(jnp.int32, (rows, 128), 1)
    at = 0 if first else 3
    one = 3 if first else 0
    tail = jnp.where((lane >= one) & (lane < one + 3), 1.0, 0.0)
    tail = jnp.where(lane == at, high.astype(F32), tail)
    tail = jnp.where(lane == at + 1, mid.astype(F32), tail)
    tail = jnp.where(lane == at + 2, low.astype(F32), tail)
    return jnp.concatenate([points, tail.astype(BF16)], axis=1)


def half_norm(points):
    wide = points.astype(F32)
    return -0.5 * jnp.sum(wide * wide, axis=1, keepdims=True)


def gelu(x):
    inner = x * (0.7978845608028654 + 0.035677408136300125 * (x * x))
    half = 0.5 * x
    return half + half * jnp.tanh(inner)


def embed_kernel(base, ids_ref, counts_ref, x_ref, w1_ref, w2_ref, w3_ref, gain_ref, *rest):
    out_ref = rest[-1]
    rows = x_ref.shape[0]
    one = gelu(jnp.dot(x_ref[...], w1_ref[...], preferred_element_type=F32)).astype(BF16)
    two = gelu(jnp.dot(one, w2_ref[...], preferred_element_type=F32)).astype(BF16)
    proj = jnp.dot(two, w3_ref[...], preferred_element_type=F32)
    mean = jnp.mean(proj * proj, axis=1, keepdims=True)
    points = (proj * lax.rsqrt(mean + 1e-06) * gain_ref[...]).astype(BF16)
    index = (base + pl.program_id(0)) * rows + lax.broadcasted_iota(jnp.int32, (rows, 1), 0)
    half = jnp.where(index < counts_ref[ids_ref[0]], half_norm(points), MASKED)
    out_ref[...] = widen(points, half, False)


def embed(base, steps, ids, counts, inputs, w_in, w_mid, w_out, gain, before=None, tile=512):
    slots = inputs.shape[0]
    whole = lambda a: pl.BlockSpec(a.shape, lambda i: (0, 0), pipeline_mode=pl.Buffered(1))
    smem = pl.BlockSpec(memory_space=pltpu.SMEM)
    more = () if before is None else (before,)
    return pl.pallas_call(
        functools.partial(embed_kernel, base),
        out_shape=jax.ShapeDtypeStruct((slots, 256), BF16),
        grid=(steps,),
        in_specs=[
            smem,
            smem,
            pl.BlockSpec((tile, inputs.shape[1]), lambda i: (i + base, 0)),
            whole(w_in),
            whole(w_mid),
            whole(w_out),
            whole(gain),
        ]
        + [pl.BlockSpec(memory_space=pl.ANY)] * len(more),
        out_specs=pl.BlockSpec((tile, 256), lambda i: (i + base, 0)),
        input_output_aliases={7: 0} if more else {},
        compiler_params=vmem(),
        cost_estimate=pl.CostEstimate(
            flops=steps * 15 * 10**8, bytes_accessed=4 << 20, transcendentals=steps << 20
        ),
        name="embed",
    )(ids, counts, inputs, w_in, w_mid, w_out, gain, *more)


WIDE = PB + 128


def panel_kernel(ids_ref, scale_ref, samples_ref, panel_ref, t_ref, pt_ref, top_ref, total, crossed):
    step = pl.program_id(0)
    i2, offset = scale_ref[0], scale_ref[1]
    share = ids_ref[1] % 4
    samples = samples_ref[...]
    panel = widen(panel_ref[...], half_norm(panel_ref[...]) + offset, True)
    mine = jnp.concatenate(
        [
            panel_ref[pl.ds(pl.multiple_of(share * 64, 64), 64), :],
            panel_ref[pl.ds(pl.multiple_of((7 - share) * 64, 64), 64), :],
        ],
        axis=0,
    )
    chunk = widen(mine, half_norm(mine) + offset, True)
    kern = jnp.exp2(i2 * lax.dot_general(samples, panel, NT, preferred_element_type=F32)).astype(BF16)
    part = jnp.exp2(i2 * lax.dot_general(chunk, samples, NT, preferred_element_type=F32)).astype(BF16)
    pt_ref[...] = kern
    sums = jnp.dot(part, kern, preferred_element_type=F32)
    cross = jnp.sum(part.astype(F32) * t_ref[...], axis=1, keepdims=True)
    cross = jnp.broadcast_to(cross, (128, 128))

    @pl.when(step == 0)
    def _():
        total[...] = sums
        crossed[...] = cross

    @pl.when(step > 0)
    def _():
        total[...] += sums
        crossed[...] += cross

    for s in range(4):

        @pl.when((step == pl.num_programs(0) - 1) & (share == s))
        def _(s=s):
            packed = jnp.concatenate(
                [
                    total[64:, : 64 * (8 - s)],
                    total[:64, : 64 * (s + 1)],
                    crossed[:64, :1],
                    crossed[64:, :1],
                    jnp.zeros((64, 62), F32),
                ],
                axis=1,
            )
            top_ref[0, :, :] = packed[:32, :]
            top_ref[1, :, :] = packed[32:, :]


def panel_top(ids, scales, samples, panel, targets, tile=512):
    slots = samples.shape[0]
    smem = pl.BlockSpec(memory_space=pltpu.SMEM)
    return pl.pallas_call(
        panel_kernel,
        out_shape=(jax.ShapeDtypeStruct((slots, PB), BF16), jax.ShapeDtypeStruct((2, 32, WIDE), F32)),
        grid=(slots // tile,),
        in_specs=[
            smem,
            smem,
            pl.BlockSpec((tile, 256), lambda i: (i, 0)),
            pl.BlockSpec(panel.shape, lambda i: (0, 0)),
            pl.BlockSpec((1, tile), lambda i: (0, i)),
        ],
        out_specs=(
            pl.BlockSpec((tile, PB), lambda i: (i, 0)),
            pl.BlockSpec((2, 32, WIDE), lambda i: (0, 0, 0)),
        ),
        scratch_shapes=[pltpu.VMEM((128, PB), F32), pltpu.VMEM((128, 128), F32)],
        compiler_params=vmem(),
        cost_estimate=pl.CostEstimate(flops=15 * 10**8, bytes_accessed=4 << 20, transcendentals=1 << 20),
        name="panel",
    )(ids, scales, samples, panel, targets)


def gram_kernel(order_ref, scale_ref, *refs):
    points_refs, (samples_ref, pt_ref, t_ref, out_ref) = refs[:4], refs[4:]
    i2, offset = scale_ref[0], scale_ref[1]
    raw = jnp.concatenate([p[...] for p in points_refs], axis=0)
    points = widen(raw, half_norm(raw) + offset, True)
    kern = jnp.exp2(
        i2 * lax.dot_general(points, samples_ref[...], NT, preferred_element_type=F32)
    ).astype(BF16)
    crossed = jnp.sum(kern.astype(F32) * t_ref[...], axis=1, keepdims=True)
    crossed = jnp.broadcast_to(crossed, (256, 128)).T
    sums = jnp.dot(kern, pt_ref[...], preferred_element_type=F32)
    for b in range(4):
        out_ref[b, :64, :] = sums[b * 64 : b * 64 + 64, :]
        out_ref[b, 64:, :] = jnp.concatenate(
            [crossed[:8, b * 64 : b * 64 + 64], jnp.zeros((8, PB - 64), F32)], axis=1
        )


def gram(order, scales, points, samples, pt, targets):
    count = order.shape[0]
    whole = lambda a: pl.BlockSpec(a.shape, lambda i, o: (0, 0), pipeline_mode=pl.Buffered(1))
    block = lambda q: pl.BlockSpec((64, 128), lambda i, o: (o[4 * i + q], 0))
    return pl.pallas_call(
        gram_kernel,
        out_shape=jax.ShapeDtypeStruct((count, 72, PB), F32),
        grid_spec=pltpu.PrefetchScalarGridSpec(
            num_scalar_prefetch=1,
            grid=(count // 4,),
            in_specs=[pl.BlockSpec(memory_space=pltpu.SMEM)]
            + [block(q) for q in range(4)]
            + [whole(samples), whole(pt), whole(targets)],
            out_specs=pl.BlockSpec((4, 72, PB), lambda i, o: (i, 0, 0)),
        ),
        compiler_params=vmem(),
        cost_estimate=pl.CostEstimate(flops=count * 2 * 10**8, bytes_accessed=6 << 20, transcendentals=2 << 20),
        name="gram",
    )(order, scales, points, points, points, points, samples, pt, targets)


def invert_block(block, store):
    groups = [block[8 * v : 8 * v + 8, :] for v in range(16)]
    lane = lax.broadcasted_iota(jnp.int32, (8, 128), 1)
    pivots = jnp.ones((8, 128), F32)
    spread = lambda a: jnp.broadcast_to(a, (8, 128))
    for g in range(16):
        j = 8 * g
        inside = (lane >= j) & (lane < j + 8)
        local = [spread(groups[g][:, j + b : j + b + 1]) for b in range(8)]
        p = [[spread(local[b][a : a + 1, :]) for b in range(a + 1)] for a in range(8)]
        cols = [[spread(groups[u][:, j + b : j + b + 1]) for b in range(8)] for u in range(g + 1, 16)]
        r = [
            jnp.where(inside, jnp.where(lane == j + a, 1.0, 0.0), spread(groups[g][a : a + 1, :]))
            for a in range(8)
        ]
        inv = []
        low = [[None] * 8 for _ in range(8)]
        for m in range(8):
            d = p[m][m]
            inv.append(1.0 / d)
            store(j + m, r[m] * lax.rsqrt(d))
            pivots = jnp.where(lane == j + m, d, pivots)
            for a in range(m + 1, 8):
                low[a][m] = p[a][m] * inv[m]
                r[a] = r[a] - low[a][m] * r[m]
                for b in range(m + 1, a):
                    p[a][b] = p[a][b] - low[a][m] * p[b][m]
                p[a][a] = p[a][a] - (p[a][m] * p[a][m]) * inv[m]
        q = [r[a] * inv[a] for a in range(8)]
        for b in range(7, 0, -1):
            for a in range(b):
                q[a] = q[a] - low[b][a] * q[b]
        for u in range(g + 1, 16):
            c = cols[u - g - 1]
            base = jnp.where(inside, 0.0, groups[u])
            for b in range(7, -1, -1):
                base = base - c[b] * q[b]
            groups[u] = base
    return pivots


def inverse_of(block, piece):
    def store(r, line):
        piece[r : r + 1, :] = line[:1, :]

    pivots = invert_block(block, store)
    row = lax.broadcasted_iota(jnp.int32, (128, 128), 0)
    lower = row >= lax.broadcasted_iota(jnp.int32, (128, 128), 1)
    return jnp.where(lower, piece[...], 0.0), jnp.log(pivots)


def factor_first_kernel(
    ids_ref, scale_ref, panel_ref, mine_ref, other_ref, inverse_ref, log_ref, left_ref, right_ref, work, piece
):
    i2, offset, over, jit = scale_ref[0], scale_ref[1], scale_ref[2], scale_ref[3]
    first = ids_ref[0] % 2 == 0
    for s in range(4):
        place = (s + 8 - ids_ref[1]) % 4
        mine, other = mine_ref[place], other_ref[place]
        share = jnp.concatenate([jnp.where(first, mine, other), jnp.where(first, other, mine)], axis=0)
        wide, slim = 64 * (8 - s), 64 * (s + 1)
        work[wide - 64 : wide, :wide] = share[:, :wide]
        work[slim - 64 : slim, :slim] = share[:, wide : wide + slim]
        if wide < PB:
            work[wide - 64 : wide, wide:] = jnp.zeros((64, PB - wide), F32)
        work[slim - 64 : slim, slim:] = jnp.zeros((64, PB - slim), F32)
        cross = share[:, PB:].T
        right_ref[:, slim - 64 : slim] = cross[64:65, :] * over
        right_ref[:, wide - 64 : wide] = cross[65:66, :] * over
    half = half_norm(panel_ref[...])
    left = widen(panel_ref[...], half + offset, True)
    right = widen(panel_ref[...], half, False)
    kern = jnp.exp2(i2 * lax.dot_general(left, right, NT, preferred_element_type=F32))
    row = lax.broadcasted_iota(jnp.int32, (PB, PB), 0)
    col = lax.broadcasted_iota(jnp.int32, (PB, PB), 1)
    lower = work[...]
    top = jnp.where(row >= col, lower, lower.T)
    work[...] = kern + jnp.where(row == col, jit, 0.0) + top * over
    t, logs = inverse_of(work[:128, :128], piece)
    rest = jnp.dot(t, work[:128, 128:], preferred_element_type=F32, precision=HI)
    u = jnp.concatenate([t, rest], axis=1)
    inverse_ref[...] = jnp.where(lax.broadcasted_iota(jnp.int32, (128, PB), 1) < 128, u, 0.0)
    away = lax.dot_general(rest, u, TN, preferred_element_type=F32, precision=HI)
    column = lax.broadcasted_iota(jnp.int32, (PB - 128, PB), 1)
    left_ref[...] = jnp.where(column < 128, 0.0, work[128:, :]) - away
    log_ref[...] = jnp.sum(logs[:1, :], axis=1, keepdims=True)


def factor_next_kernel(work_ref, inverse_ref, log_ref, work, across_ref, piece):
    work[...] = work_ref[...]
    row = lax.broadcasted_iota(jnp.int32, (PB - 128, PB), 0)
    column = lax.broadcasted_iota(jnp.int32, (PB - 128, PB), 1)

    def one(k, total):
        lo = pl.multiple_of(128 * k, 128)
        rows = pl.ds(pl.multiple_of(128 * k - 128, 128), 128)
        t, logs = inverse_of(work[rows, pl.ds(lo, 128)], piece)
        across_ref[...] = jnp.dot(t, work[rows, :], preferred_element_type=F32, precision=HI)
        across_ref[:, pl.ds(lo, 128)] = t
        u = across_ref[...]
        inverse_ref[rows, :] = jnp.where(column[:128] < lo + 128, u, 0.0)
        away = lax.dot_general(u[:, 128:], u, TN, preferred_element_type=F32, precision=HI)
        inside = (column >= lo) & (column < lo + 128)
        left = jnp.where(inside, 0.0, work[...]) - away
        work[...] = jnp.where(row >= lo, left, work[...])
        return total + logs

    total = lax.fori_loop(1, PB // 128, one, jnp.zeros((8, 128), F32))
    log_ref[...] = jnp.sum(total[:1, :], axis=1, keepdims=True)


def factor_first(ids, scales, panel, mine, other):
    full = pl.BlockSpec(memory_space=pltpu.VMEM)
    smem = pl.BlockSpec(memory_space=pltpu.SMEM)
    return pl.pallas_call(
        factor_first_kernel,
        out_shape=(
            jax.ShapeDtypeStruct((128, PB), F32),
            jax.ShapeDtypeStruct((1, 1), F32),
            jax.ShapeDtypeStruct((PB - 128, PB), F32),
            jax.ShapeDtypeStruct((1, PB), F32),
        ),
        in_specs=[smem, smem, full, full, full],
        out_specs=(full,) * 4,
        scratch_shapes=[pltpu.VMEM((PB, PB), F32), pltpu.VMEM((128, 128), F32)],
        compiler_params=vmem(),
        cost_estimate=pl.CostEstimate(flops=6 * 10**9, bytes_accessed=2 << 20, transcendentals=1 << 18),
        name="factor_first",
    )(ids, scales, panel, mine, other)


def factor_next(work):
    full = pl.BlockSpec(memory_space=pltpu.VMEM)
    return pl.pallas_call(
        factor_next_kernel,
        out_shape=(jax.ShapeDtypeStruct(work.shape, F32), jax.ShapeDtypeStruct((1, 1), F32)),
        in_specs=[full],
        out_specs=(full, full),
        scratch_shapes=[pltpu.VMEM(work.shape, F32), pltpu.VMEM((128, PB), F32), pltpu.VMEM((128, 128), F32)],
        compiler_params=vmem(),
        cost_estimate=pl.CostEstimate(flops=15 * 10**9, bytes_accessed=2 << 20, transcendentals=1 << 18),
        name="factor_next",
    )(work)


def finish_kernel(ids_ref, scale_ref, own_ref, panel_ref, right_ref, inverse0_ref, inverse1_ref, *rest):
    parts, (pf_ref, rhs_ref, sol_ref) = rest[:-3], rest[-3:]
    i2, offset, over, jit = scale_ref[0], scale_ref[1], scale_ref[2], scale_ref[3]
    rows = own_ref.shape[0]
    left = widen(own_ref[...], half_norm(own_ref[...]) + offset, True)
    right = widen(panel_ref[...], half_norm(panel_ref[...]), False)
    kern = jnp.exp2(i2 * lax.dot_general(left, right, NT, preferred_element_type=F32))
    row = ids_ref[2] + lax.broadcasted_iota(jnp.int32, (rows, PB), 0)
    col = lax.broadcasted_iota(jnp.int32, (rows, PB), 1)
    a, b, c, d = (p[...] for p in parts)
    sums = (a + b) + (c + d)
    system = kern + jnp.where(row == col, jit, 0.0) + sums[:rows, :] * over
    both = jnp.concatenate([system, jnp.broadcast_to(right_ref[...], (8, PB))], axis=0)
    inverse = jnp.concatenate([inverse0_ref[...], inverse1_ref[...]], axis=0)
    solved = lax.dot_general(both, inverse, NT, preferred_element_type=F32, precision=HI)
    pf = solved[:rows, :]
    sol = solved[rows:, :]
    pf_ref[...] = pf
    sol_ref[...] = sol[:1, :]
    back = lax.dot_general(sol, pf, NT, preferred_element_type=F32, precision=HI)
    rhs_ref[...] = sums[rows : rows + 1, :rows] * over - back[:1, :]


def finish(ids, scales, inducing, panel, *others):
    rows = inducing.shape[0] // SHARDS
    smem = pl.BlockSpec(memory_space=pltpu.SMEM)
    full = lambda a: pl.BlockSpec(a.shape, lambda i, d: (0,) * a.ndim)
    return pl.pallas_call(
        finish_kernel,
        out_shape=(
            jax.ShapeDtypeStruct((rows, PB), F32),
            jax.ShapeDtypeStruct((1, rows), F32),
            jax.ShapeDtypeStruct((1, PB), F32),
        ),
        grid_spec=pltpu.PrefetchScalarGridSpec(
            num_scalar_prefetch=1,
            grid=(1,),
            in_specs=[smem, pl.BlockSpec((rows, 128), lambda i, d: (d[0], 0))]
            + [full(a) for a in (panel,) + others],
            out_specs=(
                pl.BlockSpec((rows, PB), lambda i, d: (0, 0)),
                pl.BlockSpec((1, rows), lambda i, d: (0, 0)),
                pl.BlockSpec((1, PB), lambda i, d: (0, 0)),
            ),
        ),
        compiler_params=vmem(),
        cost_estimate=pl.CostEstimate(flops=10**9, bytes_accessed=2 << 20, transcendentals=1 << 16),
        name="finish",
    )(ids, scales, inducing, panel, *others)


def moved(x, axis, pairs):
    return lax.ppermute(x, axis, pairs)


def across(x, to):
    return lax.ppermute(x, "dp", [(i, to(i)) for i in range(SHARDS)])


def other_core(i):
    return i ^ 1


def along_x(i, k):
    return (i // 8) * 8 + (i + 2 * k) % 8


def along_y(i, k):
    return (i + 8 * k) % SHARDS


def gray(v):
    return v ^ (v >> 1)


def place_of(i):
    return i % 2, gray((i // 2) % 4), gray(i // 8)


def device_at(c, gx, gy):
    return gray(gy) * 8 + gray(gx) * 2 + c


def flipped(i, bit, which):
    c, gx, gy = place_of(i)
    return device_at(c, gx ^ (bit * (which >> 1)), gy ^ (bit * (which & 1)))


def block_order(shard):
    r = jnp.arange(SHARDS, dtype=jnp.int32)
    c, gx, gy = place_of(shard)
    gx = gx ^ (((r >> 3) & 1) | (((r >> 1) & 1) << 1))
    gy = gy ^ (((r >> 2) & 1) | ((r & 1) << 1))
    return device_at(c ^ (r >> 4), gx, gy).astype(jnp.int32)


def quarters(*parts):
    n = parts[0].shape[0] // 4
    return [sum(p[n * w : n * w + n] for p in parts) for w in range(4)]


def spread_blocks(sent, bit):
    return [sent[0]] + [
        across(sent[w], functools.partial(flipped, bit=bit, which=w)) for w in (3, 2, 1)
    ]


def after(x, *first):
    return lax.optimization_barrier((x,) + first)[0]


def sum_over(x, step):
    a, b, c = (across(x, functools.partial(step, k=k)) for k in (1, 2, 3))
    return (x + a) + (b + c)


def every_share(half):
    ring = lambda k: moved(half, "ind", [(i, (i - k) % LAYERS) for i in range(LAYERS)])
    return jnp.stack([half, ring(1), ring(2), ring(-1)])


def body(
    inputs, targets, row_counts, w_in, w_mid, w_out, feat_gain, inducing, log_scale, lengthscale, noise_var
):
    shard = lax.axis_index("dp").astype(jnp.int32)
    layer = lax.axis_index("ind").astype(jnp.int32)
    core = shard % 2
    slots = inputs.shape[0]
    own_rows = inducing.shape[0] // SHARDS
    ids = jnp.stack([shard, layer, layer * inducing.shape[0] + shard * own_rows]).astype(jnp.int32)
    order = block_order(shard)
    inv_sq = 1.0 / (lengthscale[0] * lengthscale[0])
    scales = jnp.stack(
        [inv_sq * LOG2E, log_scale[0] / inv_sq, 1.0 / noise_var[0], jnp.asarray(JITTER, F32)]
    )
    trow = targets.astype(F32).reshape(1, slots)
    network = (w_in, w_mid, w_out, feat_gain.reshape(1, -1))

    panel = inducing[:PB]
    far = [moved(panel, "ind", [(0, 3)]), moved(panel, "ind", [(0, 5)])]
    samples = embed(0, 2, ids, row_counts, inputs, *network)
    panel = jnp.where(layer == 3, far[0], jnp.where(layer == 5, far[1], panel))
    panel = after(panel, samples)
    near = [
        moved(panel, "ind", [(0, 1), (3, 4), (5, 6)]),
        moved(panel, "ind", [(0, 7), (3, 2)]),
    ]
    samples = embed(2, 2, ids, row_counts, after(inputs, panel), *network, before=samples)
    in_first = (layer == 1) | (layer == 4) | (layer == 6)
    in_second = (layer == 7) | (layer == 2)
    panel = jnp.where(in_first, near[0], jnp.where(in_second, near[1], panel))

    pt, top = panel_top(ids, scales, samples, panel, trow)
    sent = lax.dynamic_index_in_dim(top, 1 - core, 0, False)
    away = gram(after(order[16:], sent), scales, inducing, samples, pt, trow)
    half = lax.dynamic_index_in_dim(top, core, 0, False) + across(sent, other_core)
    got = across(after(away, half), other_core)
    half = after(half, away)
    half = sum_over(half, along_x)
    kept = gram(order[:16], scales, inducing, samples, pt, trow)
    half = sum_over(half, along_y)
    sums = quarters(kept, got)
    parts = spread_blocks(sums, 1)
    mine = every_share(half)
    other = across(mine, other_core)
    inverse0, log0, work, right = factor_first(ids, scales, panel, mine, other)
    parts = spread_blocks(quarters(after(parts[0], work), *parts[1:]), 2)
    inverse1, log1 = factor_next(work)
    pf, rhs, sol = finish(
        ids, scales, inducing, panel, right, inverse0, inverse1, *(p[0] for p in parts)
    )
    return pf, rhs.reshape(own_rows), sol.reshape(PB), (log0 + log1).reshape(1)


def solution(mesh):
    return jax.shard_map(
        body,
        mesh=mesh,
        in_specs=(P("dp", None), P("dp"), P(), P(), P(), P(), P(), P("ind", None), P(), P(), P()),
        out_specs=(P(("ind", "dp"), None), P(("ind", "dp")), P(), P()),
        check_vma=False,
    )
```

profile of v0, /device:TPU:0, one launch (start us, length us, event | category | flops | bytes accessed | tf_op | source)
XLA Modules:
  0.0 147.0 jit_solution(3700532755431709136)
XLA Ops:
  0.6 0.9 slice.81
  1.5 6.9 %collective-permute-start.1 = (bf16[512,128]{1,0:T(8,128)(2,1)S(1)}, bf16[512,128]{1,0:T(8,128)(2,1)S(1)}, u32[]{:S(2)}, u32[]{:S(2)}) collective-permute-start(bf16[512,128]{1,0:T(8,128)(2,1)S(1)} %slice.81), channel_id=1, source_target_pairs={{0,5},{8,13},{16,21},{24,29},{32,37},{40,45},{48,53},{56,61},{64,6... | collective-permute-start | bytes 393224 | tf_op jit(solution)/shard_map/ppermute | solution.py:407
  8.5 1.3 collective-permute-start
  9.9 0.6 pad_add_fusion.ids_ref
  10.5 0.0 copy-start.2
  10.5 7.0 %embed.2.rest_0_ = bf16[2048,256]{1,0:T(8,128)(2,1)} custom-call(s32[3]{0:T(128)} %pad_add_fusion.ids_ref, s32[32]{0:T(128)} %counts_ref.3, bf16[2048,256]{1,0:T(8,128)(2,1)} %x_ref.2, bf16[256,1024]{1,0:T(8,128)(2,1)} %w1_ref.3, bf16[1024,1024]{1,0:T(8,128)(2,1)} %w2_ref.3, bf16[1024,128]{1,0:T(8,128)(2,1)} %w3_ref.3, f32[1,128]{1,0:T(1,128)} %bitcast.31), custom_call_target="tpu_custom_call" | custom-call | flops 3000000000 | bytes 4194304 | tf_op jit(solution)/shard_map/embed/pallas_call | solution.py:70
  17.6 0.6 fusion.14
  20.2 0.6 reshape.42
  20.8 0.6 pad_maximum_fusion.1.scale_ref
  21.4 0.0 collective-permute-done.1
  21.4 0.0 collective-permute-done
  21.4 0.9 select_select_fusion.1
  22.3 1.3 collective-permute-start.3
  23.6 1.3 collective-permute-start.2
  24.9 7.1 %embed.3.samples_ref.refs_4_ = bf16[2048,256]{1,0:T(8,128)(2,1)} custom-call(s32[3]{0:T(128)} %pad_add_fusion.ids_ref, s32[32]{0:T(128)} %counts_ref.3, bf16[2048,256]{1,0:T(8,128)(2,1)} %x_ref.2, bf16[256,1024]{1,0:T(8,128)(2,1)} %w1_ref.3, bf16[1024,1024]{1,0:T(8,128)(2,1)} %w2_ref.3, bf16[1024,128]{1,0:T(8,128)(2,1)} %w3_ref.3, ...), custom_call_target="tpu_custom_call", output_to_operand_aliasing={{}: (7, {})} | custom-call | flops 3000000000 | bytes 4194304 | tf_op jit(solution)/shard_map/embed/pallas_call | solution.py:70
  32.0 0.0 collective-permute-done.3
  32.0 0.0 collective-permute-done.2
  32.0 0.7 select_select_fusion.panel_ref
  32.7 5.2 %panel.1 = (bf16[2048,512]{1,0:T(8,128)(2,1)}, f32[2,32,640]{2,1,0:T(8,128)}) custom-call(s32[3]{0:T(128)} %pad_add_fusion.ids_ref, f32[4]{0:T(128)} %pad_maximum_fusion.1.scale_ref, bf16[2048,256]{1,0:T(8,128)(2,1)} %embed.3.samples_ref.refs_4_, bf16[512,128]{1,0:T(8,128)(2,1)} %select_select_fusion.panel_ref, f32[1,2048]{1,0:T(1,128)} %bitcast.25), custom_call_target="tpu_custom_call" | custom-call | flops 1500000000 | bytes 4194304 | tf_op jit(solution)/shard_map/panel/pallas_call | solution.py:149
  37.9 0.9 dynamic-slice_bitcast_fusion
  38.8 0.0 collective-permute-start.4
  38.9 8.4 %gram.2 = f32[16,72,512]{2,1,0:T(8,128)} custom-call(s32[16]{0:T(128)} %get-tuple-element.24.order_ref, f32[4]{0:T(128)} %pad_maximum_fusion.1.scale_ref, bf16[2048,128]{1,0:T(8,128)(2,1)} %own_ref.1, bf16[2048,128]{1,0:T(8,128)(2,1)} %own_ref.1, bf16[2048,128]{1,0:T(8,128)(2,1)} %own_ref.1, bf16[2048,128]{1,0:T(8,128)(2,1)} %own_ref.1, ...), custom_call_target="tpu_custom_call" | custom-call | flops 3200000000 | bytes 6291456 | tf_op jit(solution)/shard_map/gram/pallas_call | solution.py:193
  47.3 0.0 collective-permute-done.4
  47.3 0.6 collective-permute-start.15
  47.9 2.8 %collective-permute-start.7 = (f32[32,640]{1,0:T(8,128)S(1)}, f32[32,640]{1,0:T(8,128)S(1)}, u32[]{:S(2)}, u32[]{:S(2)}) collective-permute-start(f32[32,640]{1,0:T(8,128)S(1)} %bitcast_add_fusion), channel_id=1, source_target_pairs={{0,48},{8,56},{16,0},{24,8},{32,16},{40,24},{48,32},{56,40},{64,11... | collective-permute-start | bytes 245768 | tf_op jit(solution)/shard_map/ppermute | solution.py:411
  50.7 0.8 collective-permute-start.6
  51.5 0.9 collective-permute-start.5
  52.4 2.0 %collective-permute-done.7 = f32[32,640]{1,0:T(8,128)S(1)} collective-permute-done((f32[32,640]{1,0:T(8,128)S(1)}, f32[32,640]{1,0:T(8,128)S(1)}, u32[]{:S(2)}, u32[]{:S(2)}) %collective-permute-start.7) | collective-permute-done | bytes 81952 | tf_op jit(solution)/shard_map/ppermute | solution.py:411
  54.4 2.8 %collective-permute-done.6 = f32[32,640]{1,0:T(8,128)S(1)} collective-permute-done((f32[32,640]{1,0:T(8,128)S(1)}, f32[32,640]{1,0:T(8,128)S(1)}, u32[]{:S(2)}, u32[]{:S(2)}) %collective-permute-start.6) | collective-permute-done | bytes 81952 | tf_op jit(solution)/shard_map/ppermute | solution.py:411
  57.2 0.9 collective-permute-done.5
  58.1 3.1 %collective-permute-start.10 = (f32[32,640]{1,0:T(8,128)S(1)}, f32[32,640]{1,0:T(8,128)S(1)}, u32[]{:S(2)}, u32[]{:S(2)}) collective-permute-start(f32[32,640]{1,0:T(8,128)S(1)} %add_add_fusion.1), channel_id=1, source_target_pairs={{0,192},{8,200},{16,208},{24,216},{32,224},{40,232},{48,240},{56,2... | collective-permute-start | bytes 245768 | tf_op jit(solution)/shard_map/ppermute | solution.py:411
  61.2 0.6 collective-permute-start.9
  61.9 1.0 collective-permute-start.8
  62.8 1.6 %collective-permute-done.10 = f32[32,640]{1,0:T(8,128)S(1)} collective-permute-done((f32[32,640]{1,0:T(8,128)S(1)}, f32[32,640]{1,0:T(8,128)S(1)}, u32[]{:S(2)}, u32[]{:S(2)}) %collective-permute-start.10) | collective-permute-done | bytes 81952 | tf_op jit(solution)/shard_map/ppermute | solution.py:411
  64.5 2.8 %collective-permute-done.9 = f32[32,640]{1,0:T(8,128)S(1)} collective-permute-done((f32[32,640]{1,0:T(8,128)S(1)}, f32[32,640]{1,0:T(8,128)S(1)}, u32[]{:S(2)}, u32[]{:S(2)}) %collective-permute-start.9) | collective-permute-done | bytes 81952 | tf_op jit(solution)/shard_map/ppermute | solution.py:411
  67.3 0.9 collective-permute-done.8
  68.2 0.3 collective-permute-start.13
  68.4 0.1 collective-permute-start.12
  68.5 3.1 %collective-permute-start.11 = (f32[32,640]{1,0:T(8,128)S(1)}, f32[32,640]{1,0:T(8,128)S(1)}, u32[]{:S(2)}, u32[]{:S(2)}) collective-permute-start(f32[32,640]{1,0:T(8,128)S(1)} %add_add_fusion), channel_id=1, source_target_pairs={{0,7},{1,0},{2,1},{3,2},{4,3},{5,4},{6,5},{7,6},{8,15},{9,8},{10,9... | collective-permute-start | bytes 245768 | tf_op jit(solution)/shard_map/ppermute | solution.py:407
  71.7 8.3 %gram.3 = f32[16,72,512]{2,1,0:T(8,128)} custom-call(s32[16]{0:T(128)} %get-tuple-element.46.order_ref, f32[4]{0:T(128)} %pad_maximum_fusion.1.scale_ref, bf16[2048,128]{1,0:T(8,128)(2,1)} %own_ref.1, bf16[2048,128]{1,0:T(8,128)(2,1)} %own_ref.1, bf16[2048,128]{1,0:T(8,128)(2,1)} %own_ref.1, bf16[2048,128]{1,0:T(8,128)(2,1)} %own_ref.1, ...), custom_call_target="tpu_custom_call" | custom-call | flops 3200000000 | bytes 6291456 | tf_op jit(solution)/shard_map/gram/pallas_call | solution.py:193
  80.0 0.0 collective-permute-done.13
  80.0 0.0 collective-permute-done.12
  80.0 0.0 collective-permute-done.11
  80.0 0.1 collective-permute-start.14
  80.1 0.0 collective-permute-done.15
  80.2 3.0 %slice_add_fusion.3 = (f32[4,72,512]{2,1,0:T(8,128)S(1)}, f32[4,72,512]{2,1,0:T(8,128)}, f32[4,72,512]{2,1,0:T(8,128)S(1)}, f32[4,72,512]{2,1,0:T(8,128)S(1)}) fusion(f32[16,72,512]{2,1,0:T(8,128)S(1)} %collective-permute-done.15, f32[16,72,512]{2,1,0:T(8,128)} %gram.3), kind=kLoop, calls=%fused_computation.3 | loop fusion | flops 589824 | bytes 7077888 | tf_op jit(solution)/shard_map/add | solution.py:453
  83.2 0.0 collective-permute-start.18
  83.2 0.0 collective-permute-start.17
  83.2 3.5 %collective-permute-start.16 = (f32[4,72,512]{2,1,0:T(8,128)S(1)}, f32[4,72,512]{2,1,0:T(8,128)S(1)}, u32[]{:S(2)}, u32[]{:S(2)}) collective-permute-start(f32[4,72,512]{2,1,0:T(8,128)S(1)} %get-tuple-element.41), channel_id=1, source_target_pairs={{0,80},{8,88},{16,64},{24,72},{32,112},{40,120},{48,96},{56,104},{... | collective-permute-start | bytes 1769480 | tf_op jit(solution)/shard_map/ppermute | solution.py:411
  86.7 0.0 collective-permute-done.14.other_ref
  86.7 8.5 %factor_first.1 = (f32[128,512]{1,0:T(8,128)}, f32[1,1]{1,0:T(1,128)}, f32[384,512]{1,0:T(8,128)}, f32[1,512]{1,0:T(1,128)}) custom-call(s32[3]{0:T(128)} %pad_add_fusion.ids_ref, f32[4]{0:T(128)} %pad_maximum_fusion.1.scale_ref, bf16[512,128]{1,0:T(8,128)(2,1)} %select_select_fusion.panel_ref, f32[4,32,640]{2,1,0:T(8,128)} %copy-done, ...), custom_call_target="tpu_custom_call" | custom-call | flops 6000000000 | bytes 2097152 | tf_op jit(solution)/shard_map/factor_first/pallas_call | solution.py:324
  95.2 3.9 %collective-permute-done.18 = f32[4,72,512]{2,1,0:T(8,128)S(1)} collective-permute-done((f32[4,72,512]{2,1,0:T(8,128)}, f32[4,72,512]{2,1,0:T(8,128)S(1)}, u32[]{:S(2)}, u32[]{:S(2)}) %collective-permute-start.18) | collective-permute-done | bytes 589856 | tf_op jit(solution)/shard_map/ppermute | solution.py:411
  99.1 0.3 collective-permute-done.17
  99.4 13.3 %collective-permute-done.16 = f32[4,72,512]{2,1,0:T(8,128)S(1)} collective-permute-done((f32[4,72,512]{2,1,0:T(8,128)S(1)}, f32[4,72,512]{2,1,0:T(8,128)S(1)}, u32[]{:S(2)}, u32[]{:S(2)}) %collective-permute-start.16) | collective-permute-done | bytes 589856 | tf_op jit(solution)/shard_map/ppermute | solution.py:411
  112.7 0.9 slice_add_fusion.4
  113.6 0.6 collective-permute-start.21
  114.2 0.5 collective-permute-start.20
  114.7 4.9 %collective-permute-start.19 = (f32[1,72,512]{2,1,0:T(8,128)S(1)}, f32[1,72,512]{2,1,0:T(8,128)S(1)}, u32[]{:S(2)}, u32[]{:S(2)}) collective-permute-start(f32[1,72,512]{2,1,0:T(8,128)S(1)} %get-tuple-element.44), channel_id=1, source_target_pairs={{0,240},{8,248},{16,224},{24,232},{32,208},{40,216},{48,192},{56,2... | collective-permute-start | bytes 442376 | tf_op jit(solution)/shard_map/ppermute | solution.py:411
  119.6 19.9 %factor_next.1 = (f32[384,512]{1,0:T(8,128)}, f32[1,1]{1,0:T(1,128)}) custom-call(f32[384,512]{1,0:T(8,128)} %get-tuple-element.29.work_ref), custom_call_target="tpu_custom_call" | custom-call | flops 15000000512 | bytes 2097152 | tf_op jit(solution)/shard_map/factor_next/pallas_call | solution.py:343
  140.8 0.0 collective-permute-done.20
  140.8 0.6 copy-done.3
  141.4 0.1 copy-done.4
  141.5 0.1 copy-done.5
  141.6 4.3 %finish.1 = (f32[64,512]{1,0:T(8,128)}, f32[1,64]{1,0:T(1,128)}, f32[1,512]{1,0:T(1,128)}) custom-call(s32[3]{0:T(128)} %pad_add_fusion.ids_ref, f32[4]{0:T(128)} %pad_maximum_fusion.1.scale_ref, bf16[2048,128]{1,0:T(8,128)(2,1)} %own_ref.1, bf16[512,128]{1,0:T(8,128)(2,1)} %select_select_fusion.panel_ref, f32[1,512]{1,0:T(1,128)} %get-tuple-element.27.right_ref, ...), custom_call_target="tpu_custom_call" | custom-call | flops 1000000000 | bytes 2097152 | tf_op jit(solution)/shard_map/finish/pallas_call | solution.py:382
  (15 shorter events, 0.1 us)
Async XLA Ops:
  1.5 19.8 %collective-permute-start.1 = (bf16[512,128]{1,0:T(8,128)(2,1)S(1)}, bf16[512,128]{1,0:T(8,128)(2,1)S(1)}, u32[]{:S(2)}, u32[]{:S(2)}) collective-permute-start(bf16[512,128]{1,0:T(8,128)(2,1)S(1)} %slice.81), channel_id=1, source_target_pairs={{0,5},{8,13},{16,21},{24,29},{32,37},{40,45},{48,53},{56,61},{64,6... | collective-permute-start | bytes 393224 | tf_op jit(solution)/shard_map/ppermute | solution.py:407
  8.5 12.9 %collective-permute-start = (bf16[512,128]{1,0:T(8,128)(2,1)S(1)}, bf16[512,128]{1,0:T(8,128)(2,1)S(1)}, u32[]{:S(2)}, u32[]{:S(2)}) collective-permute-start(bf16[512,128]{1,0:T(8,128)(2,1)S(1)} %slice.81), channel_id=1, source_target_pairs={{0,3},{8,11},{16,19},{24,27},{32,35},{40,43},{48,51},{56,59},{64,6... | collective-permute-start | bytes 393224 | tf_op jit(solution)/shard_map/ppermute | solution.py:407
  10.5 9.7 %copy-start.2 = (bf16[2048]{0:T(1024)(128)(2,1)S(1)}, bf16[2048]{0:T(1024)(128)(2,1)}, u32[]{:S(2)}) copy-start(bf16[2048]{0:T(1024)(128)(2,1)} %param.12) | copy-start | bytes 12292
  22.3 9.7 %collective-permute-start.3 = (bf16[512,128]{1,0:T(8,128)(2,1)S(1)}, bf16[512,128]{1,0:T(8,128)(2,1)S(1)}, u32[]{:S(2)}, u32[]{:S(2)}) collective-permute-start(bf16[512,128]{1,0:T(8,128)(2,1)S(1)} %select_select_fusion.1), channel_id=1, source_target_pairs={{0,7},{3,2},{8,15},{11,10},{16,23},{19,18},{24,31},{27,26},{32,39}... | collective-permute-start | bytes 393224 | tf_op jit(solution)/shard_map/ppermute | solution.py:407
  23.6 8.4 %collective-permute-start.2 = (bf16[512,128]{1,0:T(8,128)(2,1)S(1)}, bf16[512,128]{1,0:T(8,128)(2,1)S(1)}, u32[]{:S(2)}, u32[]{:S(2)}) collective-permute-start(bf16[512,128]{1,0:T(8,128)(2,1)S(1)} %select_select_fusion.1), channel_id=1, source_target_pairs={{0,1},{3,4},{5,6},{8,9},{11,12},{13,14},{16,17},{19,20},{21,22},{2... | collective-permute-start | bytes 393224 | tf_op jit(solution)/shard_map/ppermute | solution.py:407
  38.8 8.5 %collective-permute-start.4 = (f32[32,640]{1,0:T(8,128)S(1)}, f32[32,640]{1,0:T(8,128)S(1)}, u32[]{:S(2)}, u32[]{:S(2)}) collective-permute-start(f32[32,640]{1,0:T(8,128)S(1)} %dynamic-slice_bitcast_fusion), channel_id=1, source_target_pairs={{0,8},{8,0},{16,24},{24,16},{32,40},{40,32},{48,56},{56,48},{64,72... | collective-permute-start | bytes 245768 | tf_op jit(solution)/shard_map/ppermute | solution.py:411
  38.8 8.5 %copy-start.1 = (f32[2,32,640]{2,1,0:T(8,128)S(1)}, f32[2,32,640]{2,1,0:T(8,128)}, u32[]{:S(2)}) copy-start(f32[2,32,640]{2,1,0:T(8,128)} %get-tuple-element.23) | copy-start | bytes 491524
  47.3 32.8 %collective-permute-start.15 = (f32[16,72,512]{2,1,0:T(8,128)}, f32[16,72,512]{2,1,0:T(8,128)S(1)}, u32[]{:S(2)}, u32[]{:S(2)}) collective-permute-start(f32[16,72,512]{2,1,0:T(8,128)} %gram.2), channel_id=1, source_target_pairs={{0,8},{8,0},{16,24},{24,16},{32,40},{40,32},{48,56},{56,48},{64,72... | collective-permute-start | bytes 7077896 | tf_op jit(solution)/shard_map/ppermute | solution.py:411
  47.9 6.5 %collective-permute-start.7 = (f32[32,640]{1,0:T(8,128)S(1)}, f32[32,640]{1,0:T(8,128)S(1)}, u32[]{:S(2)}, u32[]{:S(2)}) collective-permute-start(f32[32,640]{1,0:T(8,128)S(1)} %bitcast_add_fusion), channel_id=1, source_target_pairs={{0,48},{8,56},{16,0},{24,8},{32,16},{40,24},{48,32},{56,40},{64,11... | collective-permute-start | bytes 245768 | tf_op jit(solution)/shard_map/ppermute | solution.py:411
  50.7 6.5 %collective-permute-start.6 = (f32[32,640]{1,0:T(8,128)S(1)}, f32[32,640]{1,0:T(8,128)S(1)}, u32[]{:S(2)}, u32[]{:S(2)}) collective-permute-start(f32[32,640]{1,0:T(8,128)S(1)} %bitcast_add_fusion), channel_id=1, source_target_pairs={{0,32},{8,40},{16,48},{24,56},{32,0},{40,8},{48,16},{56,24},{64,96... | collective-permute-start | bytes 245768 | tf_op jit(solution)/shard_map/ppermute | solution.py:411
  51.5 6.6 %collective-permute-start.5 = (f32[32,640]{1,0:T(8,128)S(1)}, f32[32,640]{1,0:T(8,128)S(1)}, u32[]{:S(2)}, u32[]{:S(2)}) collective-permute-start(f32[32,640]{1,0:T(8,128)S(1)} %bitcast_add_fusion), channel_id=1, source_target_pairs={{0,16},{8,24},{16,32},{24,40},{32,48},{40,56},{48,0},{56,8},{64,80... | collective-permute-start | bytes 245768 | tf_op jit(solution)/shard_map/ppermute | solution.py:411
  58.1 6.3 %collective-permute-start.10 = (f32[32,640]{1,0:T(8,128)S(1)}, f32[32,640]{1,0:T(8,128)S(1)}, u32[]{:S(2)}, u32[]{:S(2)}) collective-permute-start(f32[32,640]{1,0:T(8,128)S(1)} %add_add_fusion.1), channel_id=1, source_target_pairs={{0,192},{8,200},{16,208},{24,216},{32,224},{40,232},{48,240},{56,2... | collective-permute-start | bytes 245768 | tf_op jit(solution)/shard_map/ppermute | solution.py:411
  61.2 6.0 %collective-permute-start.9 = (f32[32,640]{1,0:T(8,128)S(1)}, f32[32,640]{1,0:T(8,128)S(1)}, u32[]{:S(2)}, u32[]{:S(2)}) collective-permute-start(f32[32,640]{1,0:T(8,128)S(1)} %add_add_fusion.1), channel_id=1, source_target_pairs={{0,128},{8,136},{16,144},{24,152},{32,160},{40,168},{48,176},{56,1... | collective-permute-start | bytes 245768 | tf_op jit(solution)/shard_map/ppermute | solution.py:411
  61.9 6.3 %collective-permute-start.8 = (f32[32,640]{1,0:T(8,128)S(1)}, f32[32,640]{1,0:T(8,128)S(1)}, u32[]{:S(2)}, u32[]{:S(2)}) collective-permute-start(f32[32,640]{1,0:T(8,128)S(1)} %add_add_fusion.1), channel_id=1, source_target_pairs={{0,64},{8,72},{16,80},{24,88},{32,96},{40,104},{48,112},{56,120},{... | collective-permute-start | bytes 245768 | tf_op jit(solution)/shard_map/ppermute | solution.py:411
  68.2 11.8 %collective-permute-start.13 = (f32[32,640]{1,0:T(8,128)S(1)}, f32[32,640]{1,0:T(8,128)S(1)}, u32[]{:S(2)}, u32[]{:S(2)}) collective-permute-start(f32[32,640]{1,0:T(8,128)S(1)} %add_add_fusion), channel_id=1, source_target_pairs={{0,1},{1,2},{2,3},{3,4},{4,5},{5,6},{6,7},{7,0},{8,9},{9,10},{10,1... | collective-permute-start | bytes 245768 | tf_op jit(solution)/shard_map/ppermute | solution.py:407
  68.4 11.6 %collective-permute-start.12 = (f32[32,640]{1,0:T(8,128)S(1)}, f32[32,640]{1,0:T(8,128)S(1)}, u32[]{:S(2)}, u32[]{:S(2)}) collective-permute-start(f32[32,640]{1,0:T(8,128)S(1)} %add_add_fusion), channel_id=1, source_target_pairs={{0,6},{1,7},{2,0},{3,1},{4,2},{5,3},{6,4},{7,5},{8,14},{9,15},{10,... | collective-permute-start | bytes 245768 | tf_op jit(solution)/shard_map/ppermute | solution.py:407
  68.5 11.5 %collective-permute-start.11 = (f32[32,640]{1,0:T(8,128)S(1)}, f32[32,640]{1,0:T(8,128)S(1)}, u32[]{:S(2)}, u32[]{:S(2)}) collective-permute-start(f32[32,640]{1,0:T(8,128)S(1)} %add_add_fusion), channel_id=1, source_target_pairs={{0,7},{1,0},{2,1},{3,2},{4,3},{5,4},{6,5},{7,6},{8,15},{9,8},{10,9... | collective-permute-start | bytes 245768 | tf_op jit(solution)/shard_map/ppermute | solution.py:407
  80.0 3.2 %copy-start = (f32[4,32,640]{2,1,0:T(8,128)}, f32[4,32,640]{2,1,0:T(8,128)S(1)}, u32[]{:S(2)}) copy-start(f32[4,32,640]{2,1,0:T(8,128)S(1)} %pad_maximum_fusion.mine_ref) | copy-start | bytes 983044
  80.0 6.6 %collective-permute-start.14 = (f32[4,32,640]{2,1,0:T(8,128)S(1)}, f32[4,32,640]{2,1,0:T(8,128)}, u32[]{:S(2)}, u32[]{:S(2)}) collective-permute-start(f32[4,32,640]{2,1,0:T(8,128)S(1)} %pad_maximum_fusion.mine_ref), channel_id=1, source_target_pairs={{0,8},{8,0},{16,24},{24,16},{32,40},{40,32},{48,56},{56,48},{64,72... | collective-permute-start | bytes 983048 | tf_op jit(solution)/shard_map/ppermute | solution.py:411
  83.2 15.9 %collective-permute-start.18 = (f32[4,72,512]{2,1,0:T(8,128)}, f32[4,72,512]{2,1,0:T(8,128)S(1)}, u32[]{:S(2)}, u32[]{:S(2)}) collective-permute-start(f32[4,72,512]{2,1,0:T(8,128)} %get-tuple-element.39), channel_id=1, source_target_pairs={{0,64},{8,72},{16,80},{24,88},{32,96},{40,104},{48,112},{56,120},{... | collective-permute-start | bytes 1769480 | tf_op jit(solution)/shard_map/ppermute | solution.py:411
  83.2 16.2 %collective-permute-start.17 = (f32[4,72,512]{2,1,0:T(8,128)S(1)}, f32[4,72,512]{2,1,0:T(8,128)S(1)}, u32[]{:S(2)}, u32[]{:S(2)}) collective-permute-start(f32[4,72,512]{2,1,0:T(8,128)S(1)} %get-tuple-element.40), channel_id=1, source_target_pairs={{0,16},{8,24},{16,0},{24,8},{32,48},{40,56},{48,32},{56,40},{64,80... | collective-permute-start | bytes 1769480 | tf_op jit(solution)/shard_map/ppermute | solution.py:411
  83.2 29.5 %collective-permute-start.16 = (f32[4,72,512]{2,1,0:T(8,128)S(1)}, f32[4,72,512]{2,1,0:T(8,128)S(1)}, u32[]{:S(2)}, u32[]{:S(2)}) collective-permute-start(f32[4,72,512]{2,1,0:T(8,128)S(1)} %get-tuple-element.41), channel_id=1, source_target_pairs={{0,80},{8,88},{16,64},{24,72},{32,112},{40,120},{48,96},{56,104},{... | collective-permute-start | bytes 1769480 | tf_op jit(solution)/shard_map/ppermute | solution.py:411
  113.6 27.1 %collective-permute-start.21 = (f32[1,72,512]{2,1,0:T(8,128)S(1)}, f32[1,72,512]{2,1,0:T(8,128)S(1)}, u32[]{:S(2)}, u32[]{:S(2)}) collective-permute-start(f32[1,72,512]{2,1,0:T(8,128)S(1)} %get-tuple-element.42), channel_id=1, source_target_pairs={{0,192},{8,200},{16,208},{24,216},{32,224},{40,232},{48,240},{56,2... | collective-permute-start | bytes 442376 | tf_op jit(solution)/shard_map/ppermute | solution.py:411
  114.2 26.6 %collective-permute-start.20 = (f32[1,72,512]{2,1,0:T(8,128)S(1)}, f32[1,72,512]{2,1,0:T(8,128)S(1)}, u32[]{:S(2)}, u32[]{:S(2)}) collective-permute-start(f32[1,72,512]{2,1,0:T(8,128)S(1)} %get-tuple-element.43), channel_id=1, source_target_pairs={{0,48},{8,56},{16,32},{24,40},{32,16},{40,24},{48,0},{56,8},{64,11... | collective-permute-start | bytes 442376 | tf_op jit(solution)/shard_map/ppermute | solution.py:411
  114.7 26.1 %collective-permute-start.19 = (f32[1,72,512]{2,1,0:T(8,128)S(1)}, f32[1,72,512]{2,1,0:T(8,128)S(1)}, u32[]{:S(2)}, u32[]{:S(2)}) collective-permute-start(f32[1,72,512]{2,1,0:T(8,128)S(1)} %get-tuple-element.44), channel_id=1, source_target_pairs={{0,240},{8,248},{16,224},{24,232},{32,208},{40,216},{48,192},{56,2... | collective-permute-start | bytes 442376 | tf_op jit(solution)/shard_map/ppermute | solution.py:411
  140.8 0.7 copy-start.3
  140.8 0.7 copy-start.4
  140.8 0.8 copy-start.5
where the time goes:
time: 149 us; the launch traced here: 147 us
  Pallas kernels  68.9 us (46%)
  starting transfers between devices  33.5 us (22%)
  waiting for transfers between devices  28.6 us (19%)
  other arithmetic  7.48 us (5%)
  between operations  5.38 us (4%)
  local copies, waits for them, and re-layouts  3.17 us (2%)
    ppermute x15, waiting for transfers between devices, across(): return lax.ppermute(x, 'dp', [(i, to(i)) for i in range(SHARDS)])  28.6 us
    pallas_call x1, Pallas kernels, factor_next(): pl.pallas_call(factor_next_kernel, out_shape=(jax.ShapeDtypeStruct(work.s...  19.9 us
    ppermute x15, starting transfers between devices, across(): return lax.ppermute(x, 'dp', [(i, to(i)) for i in range(SHARDS)])  19.2 us
    pallas_call x2, Pallas kernels, gram(): pl.pallas_call(gram_kernel, out_shape=jax.ShapeDtypeStruct((count, 72, PB...  16.8 us
    ppermute x7, starting transfers between devices, moved(): return lax.ppermute(x, axis, pairs)  14.3 us
    pallas_call x2, Pallas kernels, embed(): pl.pallas_call(functools.partial(embed_kernel, base), out_shape=jax.Shape...  14.1 us
    pallas_call x1, Pallas kernels, factor_first(): pl.pallas_call(factor_first_kernel, out_shape=(jax.ShapeDtypeStruct((128,...  8.5 us
    pallas_call x1, Pallas kernels, panel_top(): pl.pallas_call(panel_kernel, out_shape=(jax.ShapeDtypeStruct((slots, PB),...  5.23 us
  transfers between devices with their start and end apart: 22, of which 9 were waited for; matrix products, arithmetic and copies ran while one was open for 4% of the time, Pallas kernels for 40%

commit v1 on v0

--- a/solution.py
+++ b/solution.py
@@ -20,6 +20,15 @@
 
 def vmem(limit=60 << 20):
     return pltpu.CompilerParams(vmem_limit_bytes=limit)
+
+
+def scales(log_ref, length_ref):
+    square = length_ref[...] * length_ref[...]
+    return LOG2E / square, log_ref[...] * square
+
+
+def single():
+    return pl.BlockSpec((1, 1), lambda *at: (0, 0))
 
 
 def widen(points, half, first):
@@ -58,7 +67,7 @@
     mean = jnp.mean(proj * proj, axis=1, keepdims=True)
     points = (proj * lax.rsqrt(mean + 1e-06) * gain_ref[...]).astype(BF16)
     index = (base + pl.program_id(0)) * rows + lax.broadcasted_iota(jnp.int32, (rows, 1), 0)
-    half = jnp.where(index < counts_ref[ids_ref[0]], half_norm(points), MASKED)
+    half = jnp.where(index < counts_ref[ids_ref[32]], half_norm(points), MASKED)
     out_ref[...] = widen(points, half, False)
 
 
@@ -94,10 +103,12 @@
 WIDE = PB + 128
 
 
-def panel_kernel(ids_ref, scale_ref, samples_ref, panel_ref, t_ref, pt_ref, top_ref, total, crossed):
+def panel_kernel(
+    ids_ref, log_ref, length_ref, samples_ref, panel_ref, t_ref, pt_ref, kept_ref, sent_ref, total, crossed
+):
     step = pl.program_id(0)
-    i2, offset = scale_ref[0], scale_ref[1]
-    share = ids_ref[1] % 4
+    i2, offset = scales(log_ref, length_ref)
+    share = ids_ref[33] % 4
     samples = samples_ref[...]
     panel = widen(panel_ref[...], half_norm(panel_ref[...]) + offset, True)
     mine = jnp.concatenate(
@@ -139,38 +150,45 @@
                 ],
                 axis=1,
             )
-            top_ref[0, :, :] = packed[:32, :]
-            top_ref[1, :, :] = packed[32:, :]
-
-
-def panel_top(ids, scales, samples, panel, targets, tile=512):
+            first = ids_ref[32] % 2 == 0
+            kept_ref[...] = jnp.where(first, packed[:32, :], packed[32:, :])
+            sent_ref[...] = jnp.where(first, packed[32:, :], packed[:32, :])
+
+
+def panel_top(ids, log_scale, lengthscale, samples, panel, targets, tile=512):
     slots = samples.shape[0]
     smem = pl.BlockSpec(memory_space=pltpu.SMEM)
     return pl.pallas_call(
         panel_kernel,
-        out_shape=(jax.ShapeDtypeStruct((slots, PB), BF16), jax.ShapeDtypeStruct((2, 32, WIDE), F32)),
+        out_shape=(
+            jax.ShapeDtypeStruct((slots, PB), BF16),
+            jax.ShapeDtypeStruct((32, WIDE), F32),
+            jax.ShapeDtypeStruct((32, WIDE), F32),
+        ),
         grid=(slots // tile,),
         in_specs=[
             smem,
-            smem,
+            single(),
+            single(),
             pl.BlockSpec((tile, 256), lambda i: (i, 0)),
             pl.BlockSpec(panel.shape, lambda i: (0, 0)),
             pl.BlockSpec((1, tile), lambda i: (0, i)),
         ],
         out_specs=(
             pl.BlockSpec((tile, PB), lambda i: (i, 0)),
-            pl.BlockSpec((2, 32, WIDE), lambda i: (0, 0, 0)),
+            pl.BlockSpec((32, WIDE), lambda i: (0, 0)),
+            pl.BlockSpec((32, WIDE), lambda i: (0, 0)),
         ),
         scratch_shapes=[pltpu.VMEM((128, PB), F32), pltpu.VMEM((128, 128), F32)],
         compiler_params=vmem(),
         cost_estimate=pl.CostEstimate(flops=15 * 10**8, bytes_accessed=4 << 20, transcendentals=1 << 20),
         name="panel",
-    )(ids, scales, samples, panel, targets)
-
-
-def gram_kernel(order_ref, scale_ref, *refs):
+    )(ids, log_scale, lengthscale, samples, panel, targets)
+
+
+def gram_kernel(ids_ref, log_ref, length_ref, *refs):
     points_refs, (samples_ref, pt_ref, t_ref, out_ref) = refs[:4], refs[4:]
-    i2, offset = scale_ref[0], scale_ref[1]
+    i2, offset = scales(log_ref, length_ref)
     raw = jnp.concatenate([p[...] for p in points_refs], axis=0)
     points = widen(raw, half_norm(raw) + offset, True)
     kern = jnp.exp2(
@@ -186,17 +204,16 @@
         )
 
 
-def gram(order, scales, points, samples, pt, targets):
-    count = order.shape[0]
+def gram(ids, at, count, log_scale, lengthscale, points, samples, pt, targets):
     whole = lambda a: pl.BlockSpec(a.shape, lambda i, o: (0, 0), pipeline_mode=pl.Buffered(1))
-    block = lambda q: pl.BlockSpec((64, 128), lambda i, o: (o[4 * i + q], 0))
+    block = lambda q: pl.BlockSpec((64, 128), lambda i, o: (o[at + 4 * i + q], 0))
     return pl.pallas_call(
         gram_kernel,
         out_shape=jax.ShapeDtypeStruct((count, 72, PB), F32),
         grid_spec=pltpu.PrefetchScalarGridSpec(
             num_scalar_prefetch=1,
             grid=(count // 4,),
-            in_specs=[pl.BlockSpec(memory_space=pltpu.SMEM)]
+            in_specs=[single()] * 2
             + [block(q) for q in range(4)]
             + [whole(samples), whole(pt), whole(targets)],
             out_specs=pl.BlockSpec((4, 72, PB), lambda i, o: (i, 0, 0)),
@@ -204,7 +221,7 @@
         compiler_params=vmem(),
         cost_estimate=pl.CostEstimate(flops=count * 2 * 10**8, bytes_accessed=6 << 20, transcendentals=2 << 20),
         name="gram",
-    )(order, scales, points, points, points, points, samples, pt, targets)
+    )(ids, log_scale, lengthscale, points, points, points, points, samples, pt, targets)
 
 
 def invert_block(block, store):
@@ -259,12 +276,13 @@
 
 
 def factor_first_kernel(
-    ids_ref, scale_ref, panel_ref, mine_ref, other_ref, inverse_ref, log_ref, left_ref, right_ref, work, piece
+    ids_ref, log_ref_in, length_ref, noise_ref, panel_ref, mine_ref, other_ref, inverse_ref, log_ref, left_ref, right_ref, work, piece
 ):
-    i2, offset, over, jit = scale_ref[0], scale_ref[1], scale_ref[2], scale_ref[3]
-    first = ids_ref[0] % 2 == 0
+    i2, offset = scales(log_ref_in, length_ref)
+    over = 1.0 / noise_ref[...]
+    first = ids_ref[32] % 2 == 0
     for s in range(4):
-        place = (s + 8 - ids_ref[1]) % 4
+        place = (s + 8 - ids_ref[33]) % 4
         mine, other = mine_ref[place], other_ref[place]
         share = jnp.concatenate([jnp.where(first, mine, other), jnp.where(first, other, mine)], axis=0)
         wide, slim = 64 * (8 - s), 64 * (s + 1)
@@ -284,7 +302,7 @@
     col = lax.broadcasted_iota(jnp.int32, (PB, PB), 1)
     lower = work[...]
     top = jnp.where(row >= col, lower, lower.T)
-    work[...] = kern + jnp.where(row == col, jit, 0.0) + top * over
+    work[...] = kern + jnp.where(row == col, JITTER, 0.0) + top * over
     t, logs = inverse_of(work[:128, :128], piece)
     rest = jnp.dot(t, work[:128, 128:], preferred_element_type=F32, precision=HI)
     u = jnp.concatenate([t, rest], axis=1)
@@ -295,30 +313,42 @@
     log_ref[...] = jnp.sum(logs[:1, :], axis=1, keepdims=True)
 
 
-def factor_next_kernel(work_ref, inverse_ref, log_ref, work, across_ref, piece):
+def factor_middle_kernel(work_ref, inverse_ref, log_ref, left_ref, piece):
+    t, logs = inverse_of(work_ref[:128, 128:256], piece)
+    rest = jnp.dot(t, work_ref[:128, :], preferred_element_type=F32, precision=HI)
+    u = jnp.concatenate([rest[:, :128], t, rest[:, 256:]], axis=1)
+    inverse_ref[...] = jnp.where(lax.broadcasted_iota(jnp.int32, (128, PB), 1) < 256, u, 0.0)
+    away = lax.dot_general(u[:, 256:], u, TN, preferred_element_type=F32, precision=HI)
+    column = lax.broadcasted_iota(jnp.int32, (PB - 256, PB), 1)
+    left_ref[...] = jnp.where((column >= 128) & (column < 256), 0.0, work_ref[128:, :]) - away
+    log_ref[...] = jnp.sum(logs[:1, :], axis=1, keepdims=True)
+
+
+def factor_last_kernel(work_ref, inverse_ref, log_ref, work, across_ref, piece):
+    done = PB - work.shape[0]
     work[...] = work_ref[...]
-    row = lax.broadcasted_iota(jnp.int32, (PB - 128, PB), 0)
-    column = lax.broadcasted_iota(jnp.int32, (PB - 128, PB), 1)
+    row = done + lax.broadcasted_iota(jnp.int32, work.shape, 0)
+    column = lax.broadcasted_iota(jnp.int32, work.shape, 1)
 
     def one(k, total):
         lo = pl.multiple_of(128 * k, 128)
-        rows = pl.ds(pl.multiple_of(128 * k - 128, 128), 128)
+        rows = pl.ds(pl.multiple_of(128 * k - done, 128), 128)
         t, logs = inverse_of(work[rows, pl.ds(lo, 128)], piece)
         across_ref[...] = jnp.dot(t, work[rows, :], preferred_element_type=F32, precision=HI)
         across_ref[:, pl.ds(lo, 128)] = t
         u = across_ref[...]
         inverse_ref[rows, :] = jnp.where(column[:128] < lo + 128, u, 0.0)
-        away = lax.dot_general(u[:, 128:], u, TN, preferred_element_type=F32, precision=HI)
+        away = lax.dot_general(u[:, done:], u, TN, preferred_element_type=F32, precision=HI)
         inside = (column >= lo) & (column < lo + 128)
         left = jnp.where(inside, 0.0, work[...]) - away
-        work[...] = jnp.where(row >= lo, left, work[...])
+        work[...] = jnp.where(row >= lo + 128, left, work[...])
         return total + logs
 
-    total = lax.fori_loop(1, PB // 128, one, jnp.zeros((8, 128), F32))
+    total = lax.fori_loop(done // 128, PB // 128, one, jnp.zeros((8, 128), F32))
     log_ref[...] = jnp.sum(total[:1, :], axis=1, keepdims=True)
 
 
-def factor_first(ids, scales, panel, mine, other):
+def factor_first(ids, log_scale, lengthscale, noise_var, panel, mine, other):
     full = pl.BlockSpec(memory_space=pltpu.VMEM)
     smem = pl.BlockSpec(memory_space=pltpu.SMEM)
     return pl.pallas_call(
@@ -329,43 +359,62 @@
             jax.ShapeDtypeStruct((PB - 128, PB), F32),
             jax.ShapeDtypeStruct((1, PB), F32),
         ),
-        in_specs=[smem, smem, full, full, full],
+        in_specs=[smem] + [full] * 6,
         out_specs=(full,) * 4,
         scratch_shapes=[pltpu.VMEM((PB, PB), F32), pltpu.VMEM((128, 128), F32)],
         compiler_params=vmem(),
         cost_estimate=pl.CostEstimate(flops=6 * 10**9, bytes_accessed=2 << 20, transcendentals=1 << 18),
         name="factor_first",
-    )(ids, scales, panel, mine, other)
-
-
-def factor_next(work):
+    )(ids, log_scale, lengthscale, noise_var, panel, mine, other)
+
+
+def factor_middle(work):
     full = pl.BlockSpec(memory_space=pltpu.VMEM)
     return pl.pallas_call(
-        factor_next_kernel,
+        factor_middle_kernel,
+        out_shape=(
+            jax.ShapeDtypeStruct((128, PB), F32),
+            jax.ShapeDtypeStruct((1, 1), F32),
+            jax.ShapeDtypeStruct((PB - 256, PB), F32),
+        ),
+        in_specs=[full],
+        out_specs=(full,) * 3,
+        scratch_shapes=[pltpu.VMEM((128, 128), F32)],
+        compiler_params=vmem(),
+        cost_estimate=pl.CostEstimate(flops=5 * 10**9, bytes_accessed=2 << 20, transcendentals=1 << 18),
+        name="factor_middle",
+    )(work)
+
+
+def factor_last(work):
+    full = pl.BlockSpec(memory_space=pltpu.VMEM)
+    return pl.pallas_call(
+        factor_last_kernel,
         out_shape=(jax.ShapeDtypeStruct(work.shape, F32), jax.ShapeDtypeStruct((1, 1), F32)),
         in_specs=[full],
         out_specs=(full, full),
         scratch_shapes=[pltpu.VMEM(work.shape, F32), pltpu.VMEM((128, PB), F32), pltpu.VMEM((128, 128), F32)],
         compiler_params=vmem(),
-        cost_estimate=pl.CostEstimate(flops=15 * 10**9, bytes_accessed=2 << 20, transcendentals=1 << 18),
-        name="factor_next",
+        cost_estimate=pl.CostEstimate(flops=10 * 10**9, bytes_accessed=2 << 20, transcendentals=1 << 18),
+        name="factor_last",
     )(work)
 
 
-def finish_kernel(ids_ref, scale_ref, own_ref, panel_ref, right_ref, inverse0_ref, inverse1_ref, *rest):
-    parts, (pf_ref, rhs_ref, sol_ref) = rest[:-3], rest[-3:]
-    i2, offset, over, jit = scale_ref[0], scale_ref[1], scale_ref[2], scale_ref[3]
+def finish_kernel(ids_ref, log_ref, length_ref, noise_ref, own_ref, panel_ref, right_ref, *rest):
+    inverse_refs, parts, (pf_ref, rhs_ref, sol_ref) = rest[:3], rest[3:-3], rest[-3:]
+    i2, offset = scales(log_ref, length_ref)
+    over = 1.0 / noise_ref[...]
     rows = own_ref.shape[0]
     left = widen(own_ref[...], half_norm(own_ref[...]) + offset, True)
     right = widen(panel_ref[...], half_norm(panel_ref[...]), False)
     kern = jnp.exp2(i2 * lax.dot_general(left, right, NT, preferred_element_type=F32))
-    row = ids_ref[2] + lax.broadcasted_iota(jnp.int32, (rows, PB), 0)
+    row = ids_ref[34] + lax.broadcasted_iota(jnp.int32, (rows, PB), 0)
     col = lax.broadcasted_iota(jnp.int32, (rows, PB), 1)
     a, b, c, d = (p[...] for p in parts)
     sums = (a + b) + (c + d)
-    system = kern + jnp.where(row == col, jit, 0.0) + sums[:rows, :] * over
+    system = kern + jnp.where(row == col, JITTER, 0.0) + sums[:rows, :] * over
     both = jnp.concatenate([system, jnp.broadcast_to(right_ref[...], (8, PB))], axis=0)
-    inverse = jnp.concatenate([inverse0_ref[...], inverse1_ref[...]], axis=0)
+    inverse = jnp.concatenate([r[...] for r in inverse_refs], axis=0)
     solved = lax.dot_general(both, inverse, NT, preferred_element_type=F32, precision=HI)
     pf = solved[:rows, :]
     sol = solved[rows:, :]
@@ -375,9 +424,8 @@
     rhs_ref[...] = sums[rows : rows + 1, :rows] * over - back[:1, :]
 
 
-def finish(ids, scales, inducing, panel, *others):
+def finish(ids, log_scale, lengthscale, noise_var, inducing, panel, *others):
     rows = inducing.shape[0] // SHARDS
-    smem = pl.BlockSpec(memory_space=pltpu.SMEM)
     full = lambda a: pl.BlockSpec(a.shape, lambda i, d: (0,) * a.ndim)
     return pl.pallas_call(
         finish_kernel,
@@ -389,7 +437,7 @@
         grid_spec=pltpu.PrefetchScalarGridSpec(
             num_scalar_prefetch=1,
             grid=(1,),
-            in_specs=[smem, pl.BlockSpec((rows, 128), lambda i, d: (d[0], 0))]
+            in_specs=[single()] * 3 + [pl.BlockSpec((rows, 128), lambda i, d: (d[32], 0))]
             + [full(a) for a in (panel,) + others],
             out_specs=(
                 pl.BlockSpec((rows, PB), lambda i, d: (0, 0)),
@@ -400,7 +448,7 @@
         compiler_params=vmem(),
         cost_estimate=pl.CostEstimate(flops=10**9, bytes_accessed=2 << 20, transcendentals=1 << 16),
         name="finish",
-    )(ids, scales, inducing, panel, *others)
+    )(ids, log_scale, lengthscale, noise_var, inducing, panel, *others)
 
 
 def moved(x, axis, pairs):
@@ -440,12 +488,14 @@
     return device_at(c, gx ^ (bit * (which >> 1)), gy ^ (bit * (which & 1)))
 
 
-def block_order(shard):
-    r = jnp.arange(SHARDS, dtype=jnp.int32)
+def device_numbers(shard, layer, row):
+    n = jnp.arange(40, dtype=jnp.int32)
+    r = n & 31
     c, gx, gy = place_of(shard)
     gx = gx ^ (((r >> 3) & 1) | (((r >> 1) & 1) << 1))
     gy = gy ^ (((r >> 2) & 1) | ((r & 1) << 1))
-    return device_at(c ^ (r >> 4), gx, gy).astype(jnp.int32)
+    order = device_at(c ^ (r >> 4), gx, gy)
+    return jnp.where(n < 32, order, jnp.where(n == 32, shard, jnp.where(n == 33, layer, row))).astype(jnp.int32)
 
 
 def quarters(*parts):
@@ -478,15 +528,11 @@
 ):
     shard = lax.axis_index("dp").astype(jnp.int32)
     layer = lax.axis_index("ind").astype(jnp.int32)
-    core = shard % 2
     slots = inputs.shape[0]
     own_rows = inducing.shape[0] // SHARDS
-    ids = jnp.stack([shard, layer, layer * inducing.shape[0] + shard * own_rows]).astype(jnp.int32)
-    order = block_order(shard)
-    inv_sq = 1.0 / (lengthscale[0] * lengthscale[0])
-    scales = jnp.stack(
-        [inv_sq * LOG2E, log_scale[0] / inv_sq, 1.0 / noise_var[0], jnp.asarray(JITTER, F32)]
-    )
+    ids = device_numbers(shard, layer, layer * inducing.shape[0] + shard * own_rows)
+    shape = (log_scale.reshape(1, 1), lengthscale.reshape(1, 1))
+    noise = noise_var.reshape(1, 1)
     trow = targets.astype(F32).reshape(1, slots)
     network = (w_in, w_mid, w_out, feat_gain.reshape(1, -1))
 
@@ -504,26 +550,26 @@
     in_second = (layer == 7) | (layer == 2)
     panel = jnp.where(in_first, near[0], jnp.where(in_second, near[1], panel))
 
-    pt, top = panel_top(ids, scales, samples, panel, trow)
-    sent = lax.dynamic_index_in_dim(top, 1 - core, 0, False)
-    away = gram(after(order[16:], sent), scales, inducing, samples, pt, trow)
-    half = lax.dynamic_index_in_dim(top, core, 0, False) + across(sent, other_core)
+    pt, half, sent = panel_top(ids, *shape, samples, panel, trow)
+    half = half + across(sent, other_core)
+    away = gram(ids, 16, 16, *shape, inducing, samples, pt, trow)
     got = across(after(away, half), other_core)
     half = after(half, away)
     half = sum_over(half, along_x)
-    kept = gram(order[:16], scales, inducing, samples, pt, trow)
+    kept = gram(ids, 0, 16, *shape, inducing, samples, pt, trow)
     half = sum_over(half, along_y)
     sums = quarters(kept, got)
     parts = spread_blocks(sums, 1)
     mine = every_share(half)
     other = across(mine, other_core)
-    inverse0, log0, work, right = factor_first(ids, scales, panel, mine, other)
+    inverse0, log0, work, right = factor_first(ids, *shape, noise, panel, mine, other)
+    inverse1, log1, work = factor_middle(work)
     parts = spread_blocks(quarters(after(parts[0], work), *parts[1:]), 2)
-    inverse1, log1 = factor_next(work)
+    inverse2, log2 = factor_last(work)
     pf, rhs, sol = finish(
-        ids, scales, inducing, panel, right, inverse0, inverse1, *(p[0] for p in parts)
+        ids, *shape, noise, inducing, panel, right, inverse0, inverse1, inverse2, *(p[0] for p in parts)
     )
-    return pf, rhs.reshape(own_rows), sol.reshape(PB), (log0 + log1).reshape(1)
+    return pf, rhs.reshape(own_rows), sol.reshape(PB), (log0 + log1 + log2).reshape(1)
 
 
 def solution(mesh):

time: 149 us -> 146 us (0.980)
  waiting for transfers between devices: 28.6 us -> 24.7 us
  Pallas kernels: 68.9 us -> 70.9 us
  local copies, waits for them, and re-layouts: 3.17 us -> 1.66 us
    ppermute x15, waiting for transfers between devices: 28.6 us -> 20.6 us  [across(): return lax.ppermute(x, 'dp', [(i, to(i)) for i in range(SHARDS)])]
    ppermute x7, waiting for transfers between devices: 0.02 us -> 4.12 us  [moved(): return lax.ppermute(x, axis, pairs)]
    pallas_call x1 -> x2, Pallas kernels: 19.9 us -> 21 us  [the longest x1 13.3 us: factor_last(): pl.pallas_call(factor_last_kernel, out_shape=(jax.ShapeDtypeStruct(work.s...]
  transfers between devices with their start and end apart: 22 -> 22, of which waited for: 9 -> 10; matrix products, arithmetic and copies ran while one was open for 4% -> 3% of each run, Pallas kernels for 40% -> 42%
where the time goes in v1:
time: 146 us; the launch traced here: 144 us
  Pallas kernels  70.9 us (49%)
  starting transfers between devices  33.5 us (23%)
  waiting for transfers between devices  24.7 us (17%)
  other arithmetic  7.51 us (5%)
  between operations  5.88 us (4%)
  local copies, waits for them, and re-layouts  1.66 us (1%)
    ppermute x15, waiting for transfers between devices, across(): return lax.ppermute(x, 'dp', [(i, to(i)) for i in range(SHARDS)])  20.6 us
    ppermute x15, starting transfers between devices, across(): return lax.ppermute(x, 'dp', [(i, to(i)) for i in range(SHARDS)])  19.2 us
    pallas_call x2, Pallas kernels, gram(): pl.pallas_call(gram_kernel, out_shape=jax.ShapeDtypeStruct((count, 72, PB...  17.1 us
    ppermute x7, starting transfers between devices, moved(): return lax.ppermute(x, axis, pairs)  14.3 us
    pallas_call x2, Pallas kernels, embed(): pl.pallas_call(functools.partial(embed_kernel, base), out_shape=jax.Shape...  14.1 us
    pallas_call x1, Pallas kernels, factor_last(): pl.pallas_call(factor_last_kernel, out_shape=(jax.ShapeDtypeStruct(work.s...  13.3 us
    pallas_call x1, Pallas kernels, factor_first(): pl.pallas_call(factor_first_kernel, out_shape=(jax.ShapeDtypeStruct((128,...  8.85 us
    pallas_call x1, Pallas kernels, factor_middle(): pl.pallas_call(factor_middle_kernel, out_shape=(jax.ShapeDtypeStruct((128...  7.71 us
  transfers between devices with their start and end apart: 22, of which 10 were waited for; matrix products, arithmetic and copies ran while one was open for 3% of the time, Pallas kernels for 42%

profile of v1, /device:TPU:0, one launch (start us, length us, event | category | flops | bytes accessed | tf_op | source)
XLA Modules:
  0.0 144.2 jit_solution(1100294532715069007)
XLA Ops:
  0.6 0.9 slice.75
  1.5 6.9 %collective-permute-start.1 = (bf16[512,128]{1,0:T(8,128)(2,1)S(1)}, bf16[512,128]{1,0:T(8,128)(2,1)S(1)}, u32[]{:S(2)}, u32[]{:S(2)}) collective-permute-start(bf16[512,128]{1,0:T(8,128)(2,1)S(1)} %slice.75), channel_id=1, source_target_pairs={{0,5},{8,13},{16,21},{24,29},{32,37},{40,45},{48,53},{56,61},{64,6... | collective-permute-start | bytes 393224 | tf_op jit(solution)/shard_map/ppermute | solution.py:455
  8.5 1.3 collective-permute-start
  9.9 0.5 compare_select_fusion.2.ids_ref
  10.4 7.0 %embed.2.rest_0_ = bf16[2048,256]{1,0:T(8,128)(2,1)} custom-call(s32[40]{0:T(128)} %compare_select_fusion.2.ids_ref, s32[32]{0:T(128)} %counts_ref.3, bf16[2048,256]{1,0:T(8,128)(2,1)} %x_ref.2, bf16[256,1024]{1,0:T(8,128)(2,1)} %w1_ref.3, bf16[1024,1024]{1,0:T(8,128)(2,1)} %w2_ref.3, bf16[1024,128]{1,0:T(8,128)(2,1)} %w3_ref.3, f32[1,128]{1,0:T(1,128)} %bitcast.39), custom_call_target="tpu_custom_call" | custom-call | flops 3000000000 | bytes 4194304 | tf_op jit(solution)/shard_map/embed/pallas_call | solution.py:79
  18.7 0.6 reshape.43
  19.3 0.0 collective-permute-done.1
  19.3 0.0 collective-permute-done
  19.3 0.9 select_select_fusion.1
  20.3 1.3 collective-permute-start.3
  21.6 1.3 collective-permute-start.2
  22.9 7.1 %embed.3.samples_ref.refs_4_ = bf16[2048,256]{1,0:T(8,128)(2,1)} custom-call(s32[40]{0:T(128)} %compare_select_fusion.2.ids_ref, s32[32]{0:T(128)} %counts_ref.3, bf16[2048,256]{1,0:T(8,128)(2,1)} %x_ref.2, bf16[256,1024]{1,0:T(8,128)(2,1)} %w1_ref.3, bf16[1024,1024]{1,0:T(8,128)(2,1)} %w2_ref.3, ...), custom_call_target="tpu_custom_call", output_to_operand_aliasing={{}: (7, {})} | custom-call | flops 3000000000 | bytes 4194304 | tf_op jit(solution)/shard_map/embed/pallas_call | solution.py:79
  30.0 0.0 collective-permute-done.3
  30.0 0.0 collective-permute-done.2
  30.0 0.7 select_select_fusion.panel_ref
  30.6 5.5 %panel.1 = (bf16[2048,512]{1,0:T(8,128)(2,1)}, f32[32,640]{1,0:T(8,128)}, f32[32,640]{1,0:T(8,128)}) custom-call(s32[40]{0:T(128)} %compare_select_fusion.2.ids_ref, f32[1,1]{1,0:T(1,128)} %bitcast.17.log_ref, f32[1,1]{1,0:T(1,128)} %bitcast.22.length_ref, bf16[2048,256]{1,0:T(8,128)(2,1)} %embed.3.samples_ref.refs_4_, ...), custom_call_target="tpu_custom_call" | custom-call | flops 1500000000 | bytes 4194304 | tf_op jit(solution)/shard_map/panel/pallas_call | solution.py:161
  36.2 0.1 collective-permute-start.4
  36.3 0.0 copy-start
  36.3 8.6 %gram.2 = f32[16,72,512]{2,1,0:T(8,128)} custom-call(s32[40]{0:T(128)} %compare_select_fusion.2.ids_ref, f32[1,1]{1,0:T(1,128)} %bitcast.18.log_ref, f32[1,1]{1,0:T(1,128)} %bitcast.23.length_ref, bf16[2048,128]{1,0:T(8,128)(2,1)} %own_ref.1, bf16[2048,128]{1,0:T(8,128)(2,1)} %own_ref.1, bf16[2048,128]{1,0:T(8,128)(2,1)} %own_ref.1, ...), custom_call_target="tpu_custom_call" | custom-call | flops 3200000000 | bytes 6291456 | tf_op jit(solution)/shard_map/gram/pallas_call | solution.py:210
  44.9 0.0 collective-permute-done.4
  44.9 0.6 collective-permute-start.15
  45.5 2.8 %collective-permute-start.7 = (f32[32,640]{1,0:T(8,128)S(1)}, f32[32,640]{1,0:T(8,128)S(1)}, u32[]{:S(2)}, u32[]{:S(2)}) collective-permute-start(f32[32,640]{1,0:T(8,128)S(1)} %add.98), channel_id=1, source_target_pairs={{0,48},{8,56},{16,0},{24,8},{32,16},{40,24},{48,32},{56,40},{64,11... | collective-permute-start | bytes 245768 | tf_op jit(solution)/shard_map/ppermute | solution.py:459
  48.3 0.8 collective-permute-start.6
  49.1 0.9 collective-permute-start.5
  50.0 2.1 %collective-permute-done.7 = f32[32,640]{1,0:T(8,128)S(1)} collective-permute-done((f32[32,640]{1,0:T(8,128)S(1)}, f32[32,640]{1,0:T(8,128)S(1)}, u32[]{:S(2)}, u32[]{:S(2)}) %collective-permute-start.7) | collective-permute-done | bytes 81952 | tf_op jit(solution)/shard_map/ppermute | solution.py:459
  52.0 2.8 %collective-permute-done.6 = f32[32,640]{1,0:T(8,128)S(1)} collective-permute-done((f32[32,640]{1,0:T(8,128)S(1)}, f32[32,640]{1,0:T(8,128)S(1)}, u32[]{:S(2)}, u32[]{:S(2)}) %collective-permute-start.6) | collective-permute-done | bytes 81952 | tf_op jit(solution)/shard_map/ppermute | solution.py:459
  54.8 0.9 collective-permute-done.5
  55.7 3.1 %collective-permute-start.10 = (f32[32,640]{1,0:T(8,128)S(1)}, f32[32,640]{1,0:T(8,128)S(1)}, u32[]{:S(2)}, u32[]{:S(2)}) collective-permute-start(f32[32,640]{1,0:T(8,128)S(1)} %add_add_fusion.1), channel_id=1, source_target_pairs={{0,192},{8,200},{16,208},{24,216},{32,224},{40,232},{48,240},{56,2... | collective-permute-start | bytes 245768 | tf_op jit(solution)/shard_map/ppermute | solution.py:459
  58.8 0.6 collective-permute-start.9
  59.5 1.0 collective-permute-start.8
  60.4 1.6 %collective-permute-done.10 = f32[32,640]{1,0:T(8,128)S(1)} collective-permute-done((f32[32,640]{1,0:T(8,128)S(1)}, f32[32,640]{1,0:T(8,128)S(1)}, u32[]{:S(2)}, u32[]{:S(2)}) %collective-permute-start.10) | collective-permute-done | bytes 81952 | tf_op jit(solution)/shard_map/ppermute | solution.py:459
  62.1 2.8 %collective-permute-done.9 = f32[32,640]{1,0:T(8,128)S(1)} collective-permute-done((f32[32,640]{1,0:T(8,128)S(1)}, f32[32,640]{1,0:T(8,128)S(1)}, u32[]{:S(2)}, u32[]{:S(2)}) %collective-permute-start.9) | collective-permute-done | bytes 81952 | tf_op jit(solution)/shard_map/ppermute | solution.py:459
  64.9 0.9 collective-permute-done.8
  65.8 0.3 collective-permute-start.13
  66.0 0.1 collective-permute-start.12
  66.1 3.1 %collective-permute-start.11 = (f32[32,640]{1,0:T(8,128)S(1)}, f32[32,640]{1,0:T(8,128)S(1)}, u32[]{:S(2)}, u32[]{:S(2)}) collective-permute-start(f32[32,640]{1,0:T(8,128)S(1)} %add_add_fusion), channel_id=1, source_target_pairs={{0,7},{1,0},{2,1},{3,2},{4,3},{5,4},{6,5},{7,6},{8,15},{9,8},{10,9... | collective-permute-start | bytes 245768 | tf_op jit(solution)/shard_map/ppermute | solution.py:455
  69.9 1.8 %collective-permute-done.13 = f32[32,640]{1,0:T(8,128)S(1)} collective-permute-done((f32[32,640]{1,0:T(8,128)S(1)}, f32[32,640]{1,0:T(8,128)S(1)}, u32[]{:S(2)}, u32[]{:S(2)}) %collective-permute-start.13) | collective-permute-done | bytes 81952 | tf_op jit(solution)/shard_map/ppermute | solution.py:455
  71.7 0.6 collective-permute-done.12
  72.3 1.8 %collective-permute-done.11 = f32[32,640]{1,0:T(8,128)S(1)} collective-permute-done((f32[32,640]{1,0:T(8,128)S(1)}, f32[32,640]{1,0:T(8,128)S(1)}, u32[]{:S(2)}, u32[]{:S(2)}) %collective-permute-start.11) | collective-permute-done | bytes 81952 | tf_op jit(solution)/shard_map/ppermute | solution.py:455
  74.0 0.8 pad_maximum_fusion.mine_ref
  74.8 0.0 collective-permute-start.14
  74.8 8.5 %gram.3 = f32[16,72,512]{2,1,0:T(8,128)} custom-call(s32[40]{0:T(128)} %compare_select_fusion.2.ids_ref, f32[1,1]{1,0:T(1,128)} %bitcast.20.log_ref, f32[1,1]{1,0:T(1,128)} %bitcast.25.length_ref, bf16[2048,128]{1,0:T(8,128)(2,1)} %own_ref.1, bf16[2048,128]{1,0:T(8,128)(2,1)} %own_ref.1, bf16[2048,128]{1,0:T(8,128)(2,1)} %own_ref.1, ...), custom_call_target="tpu_custom_call" | custom-call | flops 3200000000 | bytes 6291456 | tf_op jit(solution)/shard_map/gram/pallas_call | solution.py:210
  83.3 0.0 collective-permute-done.15
  83.3 3.1 %slice_add_fusion.3 = (f32[4,72,512]{2,1,0:T(8,128)S(1)}, f32[4,72,512]{2,1,0:T(8,128)}, f32[4,72,512]{2,1,0:T(8,128)S(1)}, f32[4,72,512]{2,1,0:T(8,128)S(1)}) fusion(f32[16,72,512]{2,1,0:T(8,128)S(1)} %collective-permute-done.15, f32[16,72,512]{2,1,0:T(8,128)} %gram.3), kind=kLoop, calls=%fused_computation.3 | loop fusion | flops 589824 | bytes 7077888 | tf_op jit(solution)/shard_map/add | solution.py:503
  86.4 0.0 collective-permute-start.18
  86.4 0.0 collective-permute-start.17
  86.4 3.5 %collective-permute-start.16 = (f32[4,72,512]{2,1,0:T(8,128)S(1)}, f32[4,72,512]{2,1,0:T(8,128)S(1)}, u32[]{:S(2)}, u32[]{:S(2)}) collective-permute-start(f32[4,72,512]{2,1,0:T(8,128)S(1)} %get-tuple-element.47), channel_id=1, source_target_pairs={{0,80},{8,88},{16,64},{24,72},{32,112},{40,120},{48,96},{56,104},{... | collective-permute-start | bytes 1769480 | tf_op jit(solution)/shard_map/ppermute | solution.py:459
  89.9 0.0 collective-permute-done.14.other_ref
  89.9 8.9 %factor_first.1 = (f32[128,512]{1,0:T(8,128)}, f32[1,1]{1,0:T(1,128)}, f32[384,512]{1,0:T(8,128)}, f32[1,512]{1,0:T(1,128)}) custom-call(s32[40]{0:T(128)} %compare_select_fusion.2.ids_ref, f32[1,1]{1,0:T(1,128)} %bitcast.19.log_ref_in, f32[1,1]{1,0:T(1,128)} %bitcast.24.length_ref, f32[1,1]{1,0:T(1,128)} %bitcast.27.noise_ref, ...), custom_call_target="tpu_custom_call" | custom-call | flops 6000000000 | bytes 2097152 | tf_op jit(solution)/shard_map/factor_first/pallas_call | solution.py:354
  98.7 7.7 %factor_middle.1 = (f32[128,512]{1,0:T(8,128)}, f32[1,1]{1,0:T(1,128)}, f32[256,512]{1,0:T(8,128)}) custom-call(f32[384,512]{1,0:T(8,128)} %get-tuple-element.32.work_ref), custom_call_target="tpu_custom_call" | custom-call | flops 5000000000 | bytes 2097152 | tf_op jit(solution)/shard_map/factor_middle/pallas_call | solution.py:373
  106.4 0.0 collective-permute-done.18
  106.4 0.0 collective-permute-done.17
  106.4 9.5 %collective-permute-done.16 = f32[4,72,512]{2,1,0:T(8,128)S(1)} collective-permute-done((f32[4,72,512]{2,1,0:T(8,128)S(1)}, f32[4,72,512]{2,1,0:T(8,128)S(1)}, u32[]{:S(2)}, u32[]{:S(2)}) %collective-permute-start.16) | collective-permute-done | bytes 589856 | tf_op jit(solution)/shard_map/ppermute | solution.py:459
  115.9 0.9 slice_add_fusion.4
  116.8 0.6 collective-permute-start.21
  117.4 0.5 collective-permute-start.20
  117.8 4.9 %collective-permute-start.19 = (f32[1,72,512]{2,1,0:T(8,128)S(1)}, f32[1,72,512]{2,1,0:T(8,128)S(1)}, u32[]{:S(2)}, u32[]{:S(2)}) collective-permute-start(f32[1,72,512]{2,1,0:T(8,128)S(1)} %get-tuple-element.50), channel_id=1, source_target_pairs={{0,240},{8,248},{16,224},{24,232},{32,208},{40,216},{48,192},{56,2... | collective-permute-start | bytes 442376 | tf_op jit(solution)/shard_map/ppermute | solution.py:459
  122.7 13.3 %factor_last.1 = (f32[256,512]{1,0:T(8,128)}, f32[1,1]{1,0:T(1,128)}) custom-call(f32[256,512]{1,0:T(8,128)} %get-tuple-element.34.work_ref), custom_call_target="tpu_custom_call" | custom-call | flops 10000000000 | bytes 2097152 | tf_op jit(solution)/shard_map/factor_last/pallas_call | solution.py:391
  138.0 0.0 collective-permute-done.21
  138.0 0.0 collective-permute-done.20
  138.1 0.6 copy-done.2
  138.7 0.1 copy-done.3
  138.7 0.1 copy-done.4
  138.8 4.3 %finish.1 = (f32[64,512]{1,0:T(8,128)}, f32[1,64]{1,0:T(1,128)}, f32[1,512]{1,0:T(1,128)}) custom-call(s32[40]{0:T(128)} %compare_select_fusion.2.ids_ref, f32[1,1]{1,0:T(1,128)} %bitcast.21.log_ref, f32[1,1]{1,0:T(1,128)} %bitcast.26.length_ref, f32[1,1]{1,0:T(1,128)} %bitcast.28.noise_ref, bf16[2048,128]{1,0:T(8,128)(2,1)} %own_ref.1, ...), custom_call_target="tpu_custom_call" | custom-call | flops 1000000000 | bytes 2097152 | tf_op jit(solution)/shard_map/finish/pallas_call | solution.py:430
  (10 shorter events, 0.1 us)
Async XLA Ops:
  1.5 17.8 %collective-permute-start.1 = (bf16[512,128]{1,0:T(8,128)(2,1)S(1)}, bf16[512,128]{1,0:T(8,128)(2,1)S(1)}, u32[]{:S(2)}, u32[]{:S(2)}) collective-permute-start(bf16[512,128]{1,0:T(8,128)(2,1)S(1)} %slice.75), channel_id=1, source_target_pairs={{0,5},{8,13},{16,21},{24,29},{32,37},{40,45},{48,53},{56,61},{64,6... | collective-permute-start | bytes 393224 | tf_op jit(solution)/shard_map/ppermute | solution.py:455
  8.5 10.8 %collective-permute-start = (bf16[512,128]{1,0:T(8,128)(2,1)S(1)}, bf16[512,128]{1,0:T(8,128)(2,1)S(1)}, u32[]{:S(2)}, u32[]{:S(2)}) collective-permute-start(bf16[512,128]{1,0:T(8,128)(2,1)S(1)} %slice.75), channel_id=1, source_target_pairs={{0,3},{8,11},{16,19},{24,27},{32,35},{40,43},{48,51},{56,59},{64,6... | collective-permute-start | bytes 393224 | tf_op jit(solution)/shard_map/ppermute | solution.py:455
  10.4 8.3 %copy-start.1 = (bf16[2048]{0:T(1024)(128)(2,1)S(1)}, bf16[2048]{0:T(1024)(128)(2,1)}, u32[]{:S(2)}) copy-start(bf16[2048]{0:T(1024)(128)(2,1)} %param.12) | copy-start | bytes 12292
  20.3 9.7 %collective-permute-start.3 = (bf16[512,128]{1,0:T(8,128)(2,1)S(1)}, bf16[512,128]{1,0:T(8,128)(2,1)S(1)}, u32[]{:S(2)}, u32[]{:S(2)}) collective-permute-start(bf16[512,128]{1,0:T(8,128)(2,1)S(1)} %select_select_fusion.1), channel_id=1, source_target_pairs={{0,7},{3,2},{8,15},{11,10},{16,23},{19,18},{24,31},{27,26},{32,39}... | collective-permute-start | bytes 393224 | tf_op jit(solution)/shard_map/ppermute | solution.py:455
  21.6 8.4 %collective-permute-start.2 = (bf16[512,128]{1,0:T(8,128)(2,1)S(1)}, bf16[512,128]{1,0:T(8,128)(2,1)S(1)}, u32[]{:S(2)}, u32[]{:S(2)}) collective-permute-start(bf16[512,128]{1,0:T(8,128)(2,1)S(1)} %select_select_fusion.1), channel_id=1, source_target_pairs={{0,1},{3,4},{5,6},{8,9},{11,12},{13,14},{16,17},{19,20},{21,22},{2... | collective-permute-start | bytes 393224 | tf_op jit(solution)/shard_map/ppermute | solution.py:455
  36.2 8.7 %collective-permute-start.4 = (f32[32,640]{1,0:T(8,128)}, f32[32,640]{1,0:T(8,128)S(1)}, u32[]{:S(2)}, u32[]{:S(2)}) collective-permute-start(f32[32,640]{1,0:T(8,128)} %get-tuple-element.27), channel_id=1, source_target_pairs={{0,8},{8,0},{16,24},{24,16},{32,40},{40,32},{48,56},{56,48},{64,72... | collective-permute-start | bytes 245768 | tf_op jit(solution)/shard_map/ppermute | solution.py:459
  36.3 8.7 %copy-start = (f32[32,640]{1,0:T(8,128)S(1)}, f32[32,640]{1,0:T(8,128)}, u32[]{:S(2)}) copy-start(f32[32,640]{1,0:T(8,128)} %get-tuple-element.26) | copy-start | bytes 245764
  44.9 38.4 %collective-permute-start.15 = (f32[16,72,512]{2,1,0:T(8,128)}, f32[16,72,512]{2,1,0:T(8,128)S(1)}, u32[]{:S(2)}, u32[]{:S(2)}) collective-permute-start(f32[16,72,512]{2,1,0:T(8,128)} %gram.2), channel_id=1, source_target_pairs={{0,8},{8,0},{16,24},{24,16},{32,40},{40,32},{48,56},{56,48},{64,72... | collective-permute-start | bytes 7077896 | tf_op jit(solution)/shard_map/ppermute | solution.py:459
  45.5 6.5 %collective-permute-start.7 = (f32[32,640]{1,0:T(8,128)S(1)}, f32[32,640]{1,0:T(8,128)S(1)}, u32[]{:S(2)}, u32[]{:S(2)}) collective-permute-start(f32[32,640]{1,0:T(8,128)S(1)} %add.98), channel_id=1, source_target_pairs={{0,48},{8,56},{16,0},{24,8},{32,16},{40,24},{48,32},{56,40},{64,11... | collective-permute-start | bytes 245768 | tf_op jit(solution)/shard_map/ppermute | solution.py:459
  48.3 6.5 %collective-permute-start.6 = (f32[32,640]{1,0:T(8,128)S(1)}, f32[32,640]{1,0:T(8,128)S(1)}, u32[]{:S(2)}, u32[]{:S(2)}) collective-permute-start(f32[32,640]{1,0:T(8,128)S(1)} %add.98), channel_id=1, source_target_pairs={{0,32},{8,40},{16,48},{24,56},{32,0},{40,8},{48,16},{56,24},{64,96... | collective-permute-start | bytes 245768 | tf_op jit(solution)/shard_map/ppermute | solution.py:459
  49.1 6.6 %collective-permute-start.5 = (f32[32,640]{1,0:T(8,128)S(1)}, f32[32,640]{1,0:T(8,128)S(1)}, u32[]{:S(2)}, u32[]{:S(2)}) collective-permute-start(f32[32,640]{1,0:T(8,128)S(1)} %add.98), channel_id=1, source_target_pairs={{0,16},{8,24},{16,32},{24,40},{32,48},{40,56},{48,0},{56,8},{64,80... | collective-permute-start | bytes 245768 | tf_op jit(solution)/shard_map/ppermute | solution.py:459
  55.7 6.3 %collective-permute-start.10 = (f32[32,640]{1,0:T(8,128)S(1)}, f32[32,640]{1,0:T(8,128)S(1)}, u32[]{:S(2)}, u32[]{:S(2)}) collective-permute-start(f32[32,640]{1,0:T(8,128)S(1)} %add_add_fusion.1), channel_id=1, source_target_pairs={{0,192},{8,200},{16,208},{24,216},{32,224},{40,232},{48,240},{56,2... | collective-permute-start | bytes 245768 | tf_op jit(solution)/shard_map/ppermute | solution.py:459
  58.8 6.0 %collective-permute-start.9 = (f32[32,640]{1,0:T(8,128)S(1)}, f32[32,640]{1,0:T(8,128)S(1)}, u32[]{:S(2)}, u32[]{:S(2)}) collective-permute-start(f32[32,640]{1,0:T(8,128)S(1)} %add_add_fusion.1), channel_id=1, source_target_pairs={{0,128},{8,136},{16,144},{24,152},{32,160},{40,168},{48,176},{56,1... | collective-permute-start | bytes 245768 | tf_op jit(solution)/shard_map/ppermute | solution.py:459
  59.5 6.3 %collective-permute-start.8 = (f32[32,640]{1,0:T(8,128)S(1)}, f32[32,640]{1,0:T(8,128)S(1)}, u32[]{:S(2)}, u32[]{:S(2)}) collective-permute-start(f32[32,640]{1,0:T(8,128)S(1)} %add_add_fusion.1), channel_id=1, source_target_pairs={{0,64},{8,72},{16,80},{24,88},{32,96},{40,104},{48,112},{56,120},{... | collective-permute-start | bytes 245768 | tf_op jit(solution)/shard_map/ppermute | solution.py:459
  65.8 5.9 %collective-permute-start.13 = (f32[32,640]{1,0:T(8,128)S(1)}, f32[32,640]{1,0:T(8,128)S(1)}, u32[]{:S(2)}, u32[]{:S(2)}) collective-permute-start(f32[32,640]{1,0:T(8,128)S(1)} %add_add_fusion), channel_id=1, source_target_pairs={{0,1},{1,2},{2,3},{3,4},{4,5},{5,6},{6,7},{7,0},{8,9},{9,10},{10,1... | collective-permute-start | bytes 245768 | tf_op jit(solution)/shard_map/ppermute | solution.py:455
  66.0 6.2 %collective-permute-start.12 = (f32[32,640]{1,0:T(8,128)S(1)}, f32[32,640]{1,0:T(8,128)S(1)}, u32[]{:S(2)}, u32[]{:S(2)}) collective-permute-start(f32[32,640]{1,0:T(8,128)S(1)} %add_add_fusion), channel_id=1, source_target_pairs={{0,6},{1,7},{2,0},{3,1},{4,2},{5,3},{6,4},{7,5},{8,14},{9,15},{10,... | collective-permute-start | bytes 245768 | tf_op jit(solution)/shard_map/ppermute | solution.py:455
  66.1 7.9 %collective-permute-start.11 = (f32[32,640]{1,0:T(8,128)S(1)}, f32[32,640]{1,0:T(8,128)S(1)}, u32[]{:S(2)}, u32[]{:S(2)}) collective-permute-start(f32[32,640]{1,0:T(8,128)S(1)} %add_add_fusion), channel_id=1, source_target_pairs={{0,7},{1,0},{2,1},{3,2},{4,3},{5,4},{6,5},{7,6},{8,15},{9,8},{10,9... | collective-permute-start | bytes 245768 | tf_op jit(solution)/shard_map/ppermute | solution.py:455
  74.8 15.0 %collective-permute-start.14 = (f32[4,32,640]{2,1,0:T(8,128)}, f32[4,32,640]{2,1,0:T(8,128)}, u32[]{:S(2)}, u32[]{:S(2)}) collective-permute-start(f32[4,32,640]{2,1,0:T(8,128)} %pad_maximum_fusion.mine_ref), channel_id=1, source_target_pairs={{0,8},{8,0},{16,24},{24,16},{32,40},{40,32},{48,56},{56,48},{64,72... | collective-permute-start | bytes 983048 | tf_op jit(solution)/shard_map/ppermute | solution.py:459
  86.4 20.1 %collective-permute-start.18 = (f32[4,72,512]{2,1,0:T(8,128)}, f32[4,72,512]{2,1,0:T(8,128)S(1)}, u32[]{:S(2)}, u32[]{:S(2)}) collective-permute-start(f32[4,72,512]{2,1,0:T(8,128)} %get-tuple-element.45), channel_id=1, source_target_pairs={{0,64},{8,72},{16,80},{24,88},{32,96},{40,104},{48,112},{56,120},{... | collective-permute-start | bytes 1769480 | tf_op jit(solution)/shard_map/ppermute | solution.py:459
  86.4 20.1 %collective-permute-start.17 = (f32[4,72,512]{2,1,0:T(8,128)S(1)}, f32[4,72,512]{2,1,0:T(8,128)S(1)}, u32[]{:S(2)}, u32[]{:S(2)}) collective-permute-start(f32[4,72,512]{2,1,0:T(8,128)S(1)} %get-tuple-element.46), channel_id=1, source_target_pairs={{0,16},{8,24},{16,0},{24,8},{32,48},{40,56},{48,32},{56,40},{64,80... | collective-permute-start | bytes 1769480 | tf_op jit(solution)/shard_map/ppermute | solution.py:459
  86.4 29.6 %collective-permute-start.16 = (f32[4,72,512]{2,1,0:T(8,128)S(1)}, f32[4,72,512]{2,1,0:T(8,128)S(1)}, u32[]{:S(2)}, u32[]{:S(2)}) collective-permute-start(f32[4,72,512]{2,1,0:T(8,128)S(1)} %get-tuple-element.47), channel_id=1, source_target_pairs={{0,80},{8,88},{16,64},{24,72},{32,112},{40,120},{48,96},{56,104},{... | collective-permute-start | bytes 1769480 | tf_op jit(solution)/shard_map/ppermute | solution.py:459
  116.8 21.2 %collective-permute-start.21 = (f32[1,72,512]{2,1,0:T(8,128)S(1)}, f32[1,72,512]{2,1,0:T(8,128)S(1)}, u32[]{:S(2)}, u32[]{:S(2)}) collective-permute-start(f32[1,72,512]{2,1,0:T(8,128)S(1)} %get-tuple-element.48), channel_id=1, source_target_pairs={{0,192},{8,200},{16,208},{24,216},{32,224},{40,232},{48,240},{56,2... | collective-permute-start | bytes 442376 | tf_op jit(solution)/shard_map/ppermute | solution.py:459
  117.4 20.6 %collective-permute-start.20 = (f32[1,72,512]{2,1,0:T(8,128)S(1)}, f32[1,72,512]{2,1,0:T(8,128)S(1)}, u32[]{:S(2)}, u32[]{:S(2)}) collective-permute-start(f32[1,72,512]{2,1,0:T(8,128)S(1)} %get-tuple-element.49), channel_id=1, source_target_pairs={{0,48},{8,56},{16,32},{24,40},{32,16},{40,24},{48,0},{56,8},{64,11... | collective-permute-start | bytes 442376 | tf_op jit(solution)/shard_map/ppermute | solution.py:459
  117.8 20.2 %collective-permute-start.19 = (f32[1,72,512]{2,1,0:T(8,128)S(1)}, f32[1,72,512]{2,1,0:T(8,128)S(1)}, u32[]{:S(2)}, u32[]{:S(2)}) collective-permute-start(f32[1,72,512]{2,1,0:T(8,128)S(1)} %get-tuple-element.50), channel_id=1, source_target_pairs={{0,240},{8,248},{16,224},{24,232},{32,208},{40,216},{48,192},{56,2... | collective-permute-start | bytes 442376 | tf_op jit(solution)/shard_map/ppermute | solution.py:459
  138.0 0.6 copy-start.2
  138.0 0.7 copy-start.3
  138.0 0.7 copy-start.4

commit v2 on v1

--- a/solution.py
+++ b/solution.py
@@ -180,7 +180,7 @@
             pl.BlockSpec((32, WIDE), lambda i: (0, 0)),
         ),
         scratch_shapes=[pltpu.VMEM((128, PB), F32), pltpu.VMEM((128, 128), F32)],
-        compiler_params=vmem(),
+        compiler_params=vmem(36 << 20),
         cost_estimate=pl.CostEstimate(flops=15 * 10**8, bytes_accessed=4 << 20, transcendentals=1 << 20),
         name="panel",
     )(ids, log_scale, lengthscale, samples, panel, targets)
@@ -218,7 +218,7 @@
             + [whole(samples), whole(pt), whole(targets)],
             out_specs=pl.BlockSpec((4, 72, PB), lambda i, o: (i, 0, 0)),
         ),
-        compiler_params=vmem(),
+        compiler_params=vmem(36 << 20),
         cost_estimate=pl.CostEstimate(flops=count * 2 * 10**8, bytes_accessed=6 << 20, transcendentals=2 << 20),
         name="gram",
     )(ids, log_scale, lengthscale, points, points, points, points, samples, pt, targets)
@@ -362,7 +362,7 @@
         in_specs=[smem] + [full] * 6,
         out_specs=(full,) * 4,
         scratch_shapes=[pltpu.VMEM((PB, PB), F32), pltpu.VMEM((128, 128), F32)],
-        compiler_params=vmem(),
+        compiler_params=vmem(20 << 20),
         cost_estimate=pl.CostEstimate(flops=6 * 10**9, bytes_accessed=2 << 20, transcendentals=1 << 18),
         name="factor_first",
     )(ids, log_scale, lengthscale, noise_var, panel, mine, other)
@@ -380,7 +380,7 @@
         in_specs=[full],
         out_specs=(full,) * 3,
         scratch_shapes=[pltpu.VMEM((128, 128), F32)],
-        compiler_params=vmem(),
+        compiler_params=vmem(20 << 20),
         cost_estimate=pl.CostEstimate(flops=5 * 10**9, bytes_accessed=2 << 20, transcendentals=1 << 18),
         name="factor_middle",
     )(work)
@@ -394,14 +394,16 @@
         in_specs=[full],
         out_specs=(full, full),
         scratch_shapes=[pltpu.VMEM(work.shape, F32), pltpu.VMEM((128, PB), F32), pltpu.VMEM((128, 128), F32)],
-        compiler_params=vmem(),
+        compiler_params=vmem(20 << 20),
         cost_estimate=pl.CostEstimate(flops=10 * 10**9, bytes_accessed=2 << 20, transcendentals=1 << 18),
         name="factor_last",
     )(work)
 
 
 def finish_kernel(ids_ref, log_ref, length_ref, noise_ref, own_ref, panel_ref, right_ref, *rest):
-    inverse_refs, parts, (pf_ref, rhs_ref, sol_ref) = rest[:3], rest[3:-3], rest[-3:]
+    inverse_refs, log_refs, parts = rest[:3], rest[3:6], rest[6:-4]
+    pf_ref, rhs_ref, sol_ref, det_ref = rest[-4:]
+    det_ref[...] = log_refs[0][...] + log_refs[1][...] + log_refs[2][...]
     i2, offset = scales(log_ref, length_ref)
     over = 1.0 / noise_ref[...]
     rows = own_ref.shape[0]
@@ -433,6 +435,7 @@
             jax.ShapeDtypeStruct((rows, PB), F32),
             jax.ShapeDtypeStruct((1, rows), F32),
             jax.ShapeDtypeStruct((1, PB), F32),
+            jax.ShapeDtypeStruct((1, 1), F32),
         ),
         grid_spec=pltpu.PrefetchScalarGridSpec(
             num_scalar_prefetch=1,
@@ -443,9 +446,10 @@
                 pl.BlockSpec((rows, PB), lambda i, d: (0, 0)),
                 pl.BlockSpec((1, rows), lambda i, d: (0, 0)),
                 pl.BlockSpec((1, PB), lambda i, d: (0, 0)),
+                single(),
             ),
         ),
-        compiler_params=vmem(),
+        compiler_params=vmem(20 << 20),
         cost_estimate=pl.CostEstimate(flops=10**9, bytes_accessed=2 << 20, transcendentals=1 << 16),
         name="finish",
     )(ids, log_scale, lengthscale, noise_var, inducing, panel, *others)
@@ -520,7 +524,8 @@
 
 def every_share(half):
     ring = lambda k: moved(half, "ind", [(i, (i - k) % LAYERS) for i in range(LAYERS)])
-    return jnp.stack([half, ring(1), ring(2), ring(-1)])
+    shares = [half, ring(1), ring(2), ring(-1)]
+    return jnp.stack(shares)
 
 
 def body(
@@ -566,10 +571,10 @@
     inverse1, log1, work = factor_middle(work)
     parts = spread_blocks(quarters(after(parts[0], work), *parts[1:]), 2)
     inverse2, log2 = factor_last(work)
-    pf, rhs, sol = finish(
-        ids, *shape, noise, inducing, panel, right, inverse0, inverse1, inverse2, *(p[0] for p in parts)
+    pf, rhs, sol, det = finish(
+        ids, *shape, noise, inducing, panel, right, inverse0, inverse1, inverse2, log0, log1, log2, *(p[0] for p in parts)
     )
-    return pf, rhs.reshape(own_rows), sol.reshape(PB), (log0 + log1 + log2).reshape(1)
+    return pf, rhs.reshape(own_rows), sol.reshape(PB), det.reshape(1)
 
 
 def solution(mesh):

time: 146 us -> 129 us (0.88)
  Pallas kernels: 70.9 us -> 59.1 us
  other arithmetic: 7.51 us -> 1.48 us
  waiting for transfers between devices: 24.7 us -> 27.9 us
  between operations: 5.88 us -> 2.88 us
    pallas_call x2, Pallas kernels: 17.1 us -> 11 us  [gram(): pl.pallas_call(gram_kernel, out_shape=jax.ShapeDtypeStruct((count, 72, PB...]
    ppermute x15, waiting for transfers between devices: 20.6 us -> 23.8 us  [across(): return lax.ppermute(x, 'dp', [(i, to(i)) for i in range(SHARDS)])]
    add x2, other arithmetic: 3.95 us -> 0.82 us  [quarters(): return [sum((p[n * w:n * w + n] for p in parts)) for w in range(4)]]
    pallas_call x1, Pallas kernels: 7.71 us -> 5.83 us  [factor_middle(): pl.pallas_call(factor_middle_kernel, out_shape=(jax.ShapeDtypeStruct((128...]
    pallas_call x1, Pallas kernels: 5.54 us -> 3.89 us  [panel_top(): pl.pallas_call(panel_kernel, out_shape=(jax.ShapeDtypeStruct((slots, PB),...]
  transfers between devices with their start and end apart: 22 -> 22, of which waited for: 10 -> 10; matrix products, arithmetic and copies ran while one was open for 3% -> 1% of each run, Pallas kernels for 42% -> 40%
where the time goes in v2:
time: 129 us; the launch traced here: 127 us
  Pallas kernels  59.1 us (46%)
  starting transfers between devices  33.8 us (26%)
  waiting for transfers between devices  27.9 us (22%)
  between operations  2.88 us (2%)
  local copies, waits for them, and re-layouts  2.14 us (2%)
  other arithmetic  1.48 us (1%)
    ppermute x15, waiting for transfers between devices, across(): return lax.ppermute(x, 'dp', [(i, to(i)) for i in range(SHARDS)])  23.8 us
    ppermute x15, starting transfers between devices, across(): return lax.ppermute(x, 'dp', [(i, to(i)) for i in range(SHARDS)])  19.5 us
    ppermute x7, starting transfers between devices, moved(): return lax.ppermute(x, axis, pairs)  14.3 us
    pallas_call x2, Pallas kernels, embed(): pl.pallas_call(functools.partial(embed_kernel, base), out_shape=jax.Shape...  14.2 us
    pallas_call x1, Pallas kernels, factor_last(): pl.pallas_call(factor_last_kernel, out_shape=(jax.ShapeDtypeStruct(work.s...  12.2 us
    pallas_call x2, Pallas kernels, gram(): pl.pallas_call(gram_kernel, out_shape=jax.ShapeDtypeStruct((count, 72, PB...  11 us
    pallas_call x1, Pallas kernels, factor_first(): pl.pallas_call(factor_first_kernel, out_shape=(jax.ShapeDtypeStruct((128,...  7.47 us
    pallas_call x1, Pallas kernels, factor_middle(): pl.pallas_call(factor_middle_kernel, out_shape=(jax.ShapeDtypeStruct((128...  5.83 us
  transfers between devices with their start and end apart: 22, of which 10 were waited for; matrix products, arithmetic and copies ran while one was open for 1% of the time, Pallas kernels for 40%

profile of v2, /device:TPU:0, one launch (start us, length us, event | category | flops | bytes accessed | tf_op | source)
XLA Modules:
  0.0 127.3 jit_solution(1989798906848783767)
XLA Ops:
  0.6 0.9 slice.75
  1.5 6.9 %collective-permute-start.1 = (bf16[512,128]{1,0:T(8,128)(2,1)S(1)}, bf16[512,128]{1,0:T(8,128)(2,1)S(1)}, u32[]{:S(2)}, u32[]{:S(2)}) collective-permute-start(bf16[512,128]{1,0:T(8,128)(2,1)S(1)} %slice.75), channel_id=1, source_target_pairs={{0,5},{8,13},{16,21},{24,29},{32,37},{40,45},{48,53},{56,61},{64,6... | collective-permute-start | bytes 393224 | tf_op jit(solution)/shard_map/ppermute | solution.py:459
  8.5 1.3 %collective-permute-start = (bf16[512,128]{1,0:T(8,128)(2,1)S(1)}, bf16[512,128]{1,0:T(8,128)(2,1)S(1)}, u32[]{:S(2)}, u32[]{:S(2)}) collective-permute-start(bf16[512,128]{1,0:T(8,128)(2,1)S(1)} %slice.75), channel_id=1, source_target_pairs={{0,3},{8,11},{16,19},{24,27},{32,35},{40,43},{48,51},{56,59},{64,6... | collective-permute-start | bytes 393224 | tf_op jit(solution)/shard_map/ppermute | solution.py:459
  9.9 0.5 compare_select_fusion.2.ids_ref
  10.4 0.0 copy-start.3
  10.4 0.0 copy-start
  10.4 7.1 %embed.2.rest_0_ = bf16[2048,256]{1,0:T(8,128)(2,1)} custom-call(s32[40]{0:T(128)} %compare_select_fusion.2.ids_ref, s32[32]{0:T(128)} %counts_ref.3, bf16[2048,256]{1,0:T(8,128)(2,1)} %x_ref.2, bf16[256,1024]{1,0:T(8,128)(2,1)} %w1_ref.3, bf16[1024,1024]{1,0:T(8,128)(2,1)} %w2_ref.3, bf16[1024,128]{1,0:T(8,128)(2,1)} %w3_ref.3, f32[1,128]{1,0:T(1,128)} %bitcast.39), custom_call_target="tpu_custom_call" | custom-call | flops 3000000000 | bytes 4194304 | tf_op jit(solution)/shard_map/embed/pallas_call | solution.py:79
  18.8 0.0 copy-done.3
  18.8 0.0 collective-permute-done.1
  18.8 0.0 collective-permute-done
  18.8 0.0 copy-done
  18.9 1.3 %collective-permute-start.3 = (bf16[512,128]{1,0:T(8,128)(2,1)S(1)}, bf16[512,128]{1,0:T(8,128)(2,1)S(1)}, u32[]{:S(2)}, u32[]{:S(2)}) collective-permute-start(bf16[512,128]{1,0:T(8,128)(2,1)S(1)} %select_select_fusion.1), channel_id=1, source_target_pairs={{0,7},{3,2},{8,15},{11,10},{16,23},{19,18},{24,31},{27,26},{32,39}... | collective-permute-start | bytes 393224 | tf_op jit(solution)/shard_map/ppermute | solution.py:459
  20.2 1.3 %collective-permute-start.2 = (bf16[512,128]{1,0:T(8,128)(2,1)S(1)}, bf16[512,128]{1,0:T(8,128)(2,1)S(1)}, u32[]{:S(2)}, u32[]{:S(2)}) collective-permute-start(bf16[512,128]{1,0:T(8,128)(2,1)S(1)} %select_select_fusion.1), channel_id=1, source_target_pairs={{0,1},{3,4},{5,6},{8,9},{11,12},{13,14},{16,17},{19,20},{21,22},{2... | collective-permute-start | bytes 393224 | tf_op jit(solution)/shard_map/ppermute | solution.py:459
  21.5 7.1 %embed.3.samples_ref.refs_4_ = bf16[2048,256]{1,0:T(8,128)(2,1)} custom-call(s32[40]{0:T(128)} %compare_select_fusion.2.ids_ref, s32[32]{0:T(128)} %counts_ref.3, bf16[2048,256]{1,0:T(8,128)(2,1)} %x_ref.2, bf16[256,1024]{1,0:T(8,128)(2,1)} %w1_ref.3, bf16[1024,1024]{1,0:T(8,128)(2,1)} %w2_ref.3, ...), custom_call_target="tpu_custom_call", output_to_operand_aliasing={{}: (7, {})} | custom-call | flops 3000000000 | bytes 4194304 | tf_op jit(solution)/shard_map/embed/pallas_call | solution.py:79
  28.6 0.0 collective-permute-done.3
  28.6 0.0 collective-permute-done.2
  28.6 0.0 copy-done.1
  28.6 0.0 copy-start.2
  28.7 1.2 copy-done.2
  29.9 3.9 %panel.1 = (bf16[2048,512]{1,0:T(8,128)(2,1)S(1)}, f32[32,640]{1,0:T(8,128)S(1)}, f32[32,640]{1,0:T(8,128)S(1)}) custom-call(s32[40]{0:T(128)S(1)} %copy-done.1, f32[1,1]{1,0:T(1,128)} %bitcast.17.log_ref, f32[1,1]{1,0:T(1,128)} %bitcast.22.length_ref, bf16[2048,256]{1,0:T(8,128)(2,1)S(1)} %copy-done.2, bf16[512,128]{1,0:T(8,128)(2,1)S(1)} %select_select_fusion.panel_ref, ...), custom_call_target="tpu_custom_call" | custom-call | flops 1500000000 | bytes 4194304 | tf_op jit(solution)/shard_map/panel/pallas_call | solution.py:161
  33.8 0.1 collective-permute-start.4
  33.9 5.5 %gram.2 = f32[16,72,512]{2,1,0:T(8,128)S(1)} custom-call(s32[40]{0:T(128)S(1)} %copy-done.1, f32[1,1]{1,0:T(1,128)} %bitcast.18.log_ref, f32[1,1]{1,0:T(1,128)} %bitcast.23.length_ref, bf16[2048,128]{1,0:T(8,128)(2,1)S(1)} %copy-done, bf16[2048,128]{1,0:T(8,128)(2,1)S(1)} %copy-done, bf16[2048,128]{1,0:T(8,128)(2,1)S(1)} %copy-done, ...), custom_call_target="tpu_custom_call" | custom-call | flops 3200000000 | bytes 6291456 | tf_op jit(solution)/shard_map/gram/pallas_call | solution.py:210
  39.4 0.0 collective-permute-done.4
  39.4 0.6 collective-permute-start.15
  40.0 2.8 %collective-permute-start.7 = (f32[32,640]{1,0:T(8,128)S(1)}, f32[32,640]{1,0:T(8,128)S(1)}, u32[]{:S(2)}, u32[]{:S(2)}) collective-permute-start(f32[32,640]{1,0:T(8,128)S(1)} %add.92), channel_id=1, source_target_pairs={{0,48},{8,56},{16,0},{24,8},{32,16},{40,24},{48,32},{56,40},{64,11... | collective-permute-start | bytes 245768 | tf_op jit(solution)/shard_map/ppermute | solution.py:463
  42.7 0.8 collective-permute-start.6
  43.5 0.9 collective-permute-start.5
  44.4 2.0 %collective-permute-done.7 = f32[32,640]{1,0:T(8,128)S(1)} collective-permute-done((f32[32,640]{1,0:T(8,128)S(1)}, f32[32,640]{1,0:T(8,128)S(1)}, u32[]{:S(2)}, u32[]{:S(2)}) %collective-permute-start.7) | collective-permute-done | bytes 81952 | tf_op jit(solution)/shard_map/ppermute | solution.py:463
  46.5 2.8 %collective-permute-done.6 = f32[32,640]{1,0:T(8,128)S(1)} collective-permute-done((f32[32,640]{1,0:T(8,128)S(1)}, f32[32,640]{1,0:T(8,128)S(1)}, u32[]{:S(2)}, u32[]{:S(2)}) %collective-permute-start.6) | collective-permute-done | bytes 81952 | tf_op jit(solution)/shard_map/ppermute | solution.py:463
  49.3 0.9 collective-permute-done.5
  50.2 3.1 %collective-permute-start.10 = (f32[32,640]{1,0:T(8,128)S(1)}, f32[32,640]{1,0:T(8,128)S(1)}, u32[]{:S(2)}, u32[]{:S(2)}) collective-permute-start(f32[32,640]{1,0:T(8,128)S(1)} %add_add_fusion.1), channel_id=1, source_target_pairs={{0,192},{8,200},{16,208},{24,216},{32,224},{40,232},{48,240},{56,2... | collective-permute-start | bytes 245768 | tf_op jit(solution)/shard_map/ppermute | solution.py:463
  53.3 0.6 collective-permute-start.9
  53.9 1.0 collective-permute-start.8
  54.9 1.6 %collective-permute-done.10 = f32[32,640]{1,0:T(8,128)S(1)} collective-permute-done((f32[32,640]{1,0:T(8,128)S(1)}, f32[32,640]{1,0:T(8,128)S(1)}, u32[]{:S(2)}, u32[]{:S(2)}) %collective-permute-start.10) | collective-permute-done | bytes 81952 | tf_op jit(solution)/shard_map/ppermute | solution.py:463
  56.5 2.8 %collective-permute-done.9 = f32[32,640]{1,0:T(8,128)S(1)} collective-permute-done((f32[32,640]{1,0:T(8,128)S(1)}, f32[32,640]{1,0:T(8,128)S(1)}, u32[]{:S(2)}, u32[]{:S(2)}) %collective-permute-start.9) | collective-permute-done | bytes 81952 | tf_op jit(solution)/shard_map/ppermute | solution.py:463
  59.3 0.9 collective-permute-done.8
  60.2 0.3 collective-permute-start.13
  60.5 0.1 collective-permute-start.12
  60.6 3.1 %collective-permute-start.11 = (f32[32,640]{1,0:T(8,128)S(1)}, f32[32,640]{1,0:T(8,128)S(1)}, u32[]{:S(2)}, u32[]{:S(2)}) collective-permute-start(f32[32,640]{1,0:T(8,128)S(1)} %add_add_fusion), channel_id=1, source_target_pairs={{0,7},{1,0},{2,1},{3,2},{4,3},{5,4},{6,5},{7,6},{8,15},{9,8},{10,9... | collective-permute-start | bytes 245768 | tf_op jit(solution)/shard_map/ppermute | solution.py:459
  64.3 1.8 %collective-permute-done.13 = f32[32,640]{1,0:T(8,128)S(1)} collective-permute-done((f32[32,640]{1,0:T(8,128)S(1)}, f32[32,640]{1,0:T(8,128)S(1)}, u32[]{:S(2)}, u32[]{:S(2)}) %collective-permute-start.13) | collective-permute-done | bytes 81952 | tf_op jit(solution)/shard_map/ppermute | solution.py:459
  66.1 0.6 collective-permute-done.12
  66.7 1.7 %collective-permute-done.11 = f32[32,640]{1,0:T(8,128)S(1)} collective-permute-done((f32[32,640]{1,0:T(8,128)S(1)}, f32[32,640]{1,0:T(8,128)S(1)}, u32[]{:S(2)}, u32[]{:S(2)}) %collective-permute-start.11) | collective-permute-done | bytes 81952 | tf_op jit(solution)/shard_map/ppermute | solution.py:459
  68.5 0.1 collective-permute-start.14
  68.6 5.5 %gram.3 = f32[16,72,512]{2,1,0:T(8,128)S(1)} custom-call(s32[40]{0:T(128)S(1)} %copy-done.1, f32[1,1]{1,0:T(1,128)} %bitcast.20.log_ref, f32[1,1]{1,0:T(1,128)} %bitcast.25.length_ref, bf16[2048,128]{1,0:T(8,128)(2,1)S(1)} %copy-done, bf16[2048,128]{1,0:T(8,128)(2,1)S(1)} %copy-done, bf16[2048,128]{1,0:T(8,128)(2,1)S(1)} %copy-done, ...), custom_call_target="tpu_custom_call" | custom-call | flops 3200000000 | bytes 6291456 | tf_op jit(solution)/shard_map/gram/pallas_call | solution.py:210
  74.1 0.0 collective-permute-done.15
  74.1 0.6 slice_add_fusion.3
  74.7 0.1 collective-permute-start.18
  74.8 0.1 collective-permute-start.17
  74.9 3.4 %collective-permute-start.16 = (f32[4,72,512]{2,1,0:T(8,128)S(1)}, f32[4,72,512]{2,1,0:T(8,128)S(1)}, u32[]{:S(2)}, u32[]{:S(2)}) collective-permute-start(f32[4,72,512]{2,1,0:T(8,128)S(1)} %get-tuple-element.49), channel_id=1, source_target_pairs={{0,80},{8,88},{16,64},{24,72},{32,112},{40,120},{48,96},{56,104},{... | collective-permute-start | bytes 1769480 | tf_op jit(solution)/shard_map/ppermute | solution.py:463
  78.2 0.0 collective-permute-done.14.other_ref
  78.2 7.5 %factor_first.1 = (f32[128,512]{1,0:T(8,128)S(1)}, f32[1,1]{1,0:T(1,128)}, f32[384,512]{1,0:T(8,128)S(1)}, f32[1,512]{1,0:T(1,128)S(1)}) custom-call(s32[40]{0:T(128)S(1)} %copy-done.1, f32[1,1]{1,0:T(1,128)} %bitcast.19.log_ref_in, f32[1,1]{1,0:T(1,128)} %bitcast.24.length_ref, f32[1,1]{1,0:T(1,128)} %bitcast.27.noise_ref, ...), custom_call_target="tpu_custom_call" | custom-call | flops 6000000000 | bytes 2097152 | tf_op jit(solution)/shard_map/factor_first/pallas_call | solution.py:354
  85.7 5.8 %factor_middle.1 = (f32[128,512]{1,0:T(8,128)S(1)}, f32[1,1]{1,0:T(1,128)}, f32[256,512]{1,0:T(8,128)S(1)}) custom-call(f32[384,512]{1,0:T(8,128)S(1)} %get-tuple-element.33.work_ref), custom_call_target="tpu_custom_call" | custom-call | flops 5000000000 | bytes 2097152 | tf_op jit(solution)/shard_map/factor_middle/pallas_call | solution.py:373
  91.5 0.0 collective-permute-done.18
  91.5 0.0 collective-permute-done.17
  91.5 12.7 %collective-permute-done.16 = f32[4,72,512]{2,1,0:T(8,128)S(1)} collective-permute-done((f32[4,72,512]{2,1,0:T(8,128)S(1)}, f32[4,72,512]{2,1,0:T(8,128)S(1)}, u32[]{:S(2)}, u32[]{:S(2)}) %collective-permute-start.16) | collective-permute-done | bytes 589856 | tf_op jit(solution)/shard_map/ppermute | solution.py:463
  104.3 0.3 slice_add_fusion.4
  104.5 0.6 collective-permute-start.21
  105.2 0.5 collective-permute-start.20
  105.7 4.9 %collective-permute-start.19 = (f32[1,72,512]{2,1,0:T(8,128)S(1)}, f32[1,72,512]{2,1,0:T(8,128)S(1)}, u32[]{:S(2)}, u32[]{:S(2)}) collective-permute-start(f32[1,72,512]{2,1,0:T(8,128)S(1)} %get-tuple-element.52), channel_id=1, source_target_pairs={{0,240},{8,248},{16,224},{24,232},{32,208},{40,216},{48,192},{56,2... | collective-permute-start | bytes 442376 | tf_op jit(solution)/shard_map/ppermute | solution.py:463
  110.5 12.2 %factor_last.1 = (f32[256,512]{1,0:T(8,128)S(1)}, f32[1,1]{1,0:T(1,128)}) custom-call(f32[256,512]{1,0:T(8,128)S(1)} %get-tuple-element.35.work_ref), custom_call_target="tpu_custom_call" | custom-call | flops 10000000000 | bytes 2097152 | tf_op jit(solution)/shard_map/factor_last/pallas_call | solution.py:391
  122.8 0.0 collective-permute-done.21
  122.8 0.0 collective-permute-done.20
  122.8 0.0 collective-permute-done.19
  122.8 4.5 %finish.1 = (f32[64,512]{1,0:T(8,128)}, f32[1,64]{1,0:T(1,128)}, f32[1,512]{1,0:T(1,128)}, f32[1,1]{1,0:T(1,128)}) custom-call(s32[40]{0:T(128)S(1)} %copy-done.1, f32[1,1]{1,0:T(1,128)} %bitcast.21.log_ref, f32[1,1]{1,0:T(1,128)} %bitcast.26.length_ref, f32[1,1]{1,0:T(1,128)} %bitcast.28.noise_ref, bf16[2048,128]{1,0:T(8,128)(2,1)S(1)} %copy-done, ...), custom_call_target="tpu_custom_call" | custom-call | flops 1000000000 | bytes 2097152 | tf_op jit(solution)/shard_map/finish/pallas_call | solution.py:432
  (8 shorter events, 0.1 us)
Async XLA Ops:
  1.5 17.3 %collective-permute-start.1 = (bf16[512,128]{1,0:T(8,128)(2,1)S(1)}, bf16[512,128]{1,0:T(8,128)(2,1)S(1)}, u32[]{:S(2)}, u32[]{:S(2)}) collective-permute-start(bf16[512,128]{1,0:T(8,128)(2,1)S(1)} %slice.75), channel_id=1, source_target_pairs={{0,5},{8,13},{16,21},{24,29},{32,37},{40,45},{48,53},{56,61},{64,6... | collective-permute-start | bytes 393224 | tf_op jit(solution)/shard_map/ppermute | solution.py:459
  8.5 10.3 %collective-permute-start = (bf16[512,128]{1,0:T(8,128)(2,1)S(1)}, bf16[512,128]{1,0:T(8,128)(2,1)S(1)}, u32[]{:S(2)}, u32[]{:S(2)}) collective-permute-start(bf16[512,128]{1,0:T(8,128)(2,1)S(1)} %slice.75), channel_id=1, source_target_pairs={{0,3},{8,11},{16,19},{24,27},{32,35},{40,43},{48,51},{56,59},{64,6... | collective-permute-start | bytes 393224 | tf_op jit(solution)/shard_map/ppermute | solution.py:459
  10.4 8.4 %copy-start.3 = (bf16[2048]{0:T(1024)(128)(2,1)S(1)}, bf16[2048]{0:T(1024)(128)(2,1)}, u32[]{:S(2)}) copy-start(bf16[2048]{0:T(1024)(128)(2,1)} %param.12) | copy-start | bytes 12292
  10.4 8.5 %copy-start = (bf16[2048,128]{1,0:T(8,128)(2,1)S(1)}, bf16[2048,128]{1,0:T(8,128)(2,1)}, u32[]{:S(2)}) copy-start(bf16[2048,128]{1,0:T(8,128)(2,1)} %own_ref.1) | copy-start | bytes 1572868
  18.9 9.7 %copy-start.1 = (s32[40]{0:T(128)S(1)}, s32[40]{0:T(128)}, u32[]{:S(2)}) copy-start(s32[40]{0:T(128)} %compare_select_fusion.2.ids_ref) | copy-start | bytes 484
  18.9 9.7 %collective-permute-start.3 = (bf16[512,128]{1,0:T(8,128)(2,1)S(1)}, bf16[512,128]{1,0:T(8,128)(2,1)S(1)}, u32[]{:S(2)}, u32[]{:S(2)}) collective-permute-start(bf16[512,128]{1,0:T(8,128)(2,1)S(1)} %select_select_fusion.1), channel_id=1, source_target_pairs={{0,7},{3,2},{8,15},{11,10},{16,23},{19,18},{24,31},{27,26},{32,39}... | collective-permute-start | bytes 393224 | tf_op jit(solution)/shard_map/ppermute | solution.py:459
  20.2 8.4 %collective-permute-start.2 = (bf16[512,128]{1,0:T(8,128)(2,1)S(1)}, bf16[512,128]{1,0:T(8,128)(2,1)S(1)}, u32[]{:S(2)}, u32[]{:S(2)}) collective-permute-start(bf16[512,128]{1,0:T(8,128)(2,1)S(1)} %select_select_fusion.1), channel_id=1, source_target_pairs={{0,1},{3,4},{5,6},{8,9},{11,12},{13,14},{16,17},{19,20},{21,22},{2... | collective-permute-start | bytes 393224 | tf_op jit(solution)/shard_map/ppermute | solution.py:459
  28.6 1.2 copy-start.2
  33.8 5.6 %collective-permute-start.4 = (f32[32,640]{1,0:T(8,128)S(1)}, f32[32,640]{1,0:T(8,128)S(1)}, u32[]{:S(2)}, u32[]{:S(2)}) collective-permute-start(f32[32,640]{1,0:T(8,128)S(1)} %get-tuple-element.28), channel_id=1, source_target_pairs={{0,8},{8,0},{16,24},{24,16},{32,40},{40,32},{48,56},{56,48},{64,72... | collective-permute-start | bytes 245768 | tf_op jit(solution)/shard_map/ppermute | solution.py:463
  39.4 34.7 %collective-permute-start.15 = (f32[16,72,512]{2,1,0:T(8,128)S(1)}, f32[16,72,512]{2,1,0:T(8,128)S(1)}, u32[]{:S(2)}, u32[]{:S(2)}) collective-permute-start(f32[16,72,512]{2,1,0:T(8,128)S(1)} %gram.2), channel_id=1, source_target_pairs={{0,8},{8,0},{16,24},{24,16},{32,40},{40,32},{48,56},{56,48},{64,72... | collective-permute-start | bytes 7077896 | tf_op jit(solution)/shard_map/ppermute | solution.py:463
  40.0 6.5 %collective-permute-start.7 = (f32[32,640]{1,0:T(8,128)S(1)}, f32[32,640]{1,0:T(8,128)S(1)}, u32[]{:S(2)}, u32[]{:S(2)}) collective-permute-start(f32[32,640]{1,0:T(8,128)S(1)} %add.92), channel_id=1, source_target_pairs={{0,48},{8,56},{16,0},{24,8},{32,16},{40,24},{48,32},{56,40},{64,11... | collective-permute-start | bytes 245768 | tf_op jit(solution)/shard_map/ppermute | solution.py:463
  42.7 6.5 %collective-permute-start.6 = (f32[32,640]{1,0:T(8,128)S(1)}, f32[32,640]{1,0:T(8,128)S(1)}, u32[]{:S(2)}, u32[]{:S(2)}) collective-permute-start(f32[32,640]{1,0:T(8,128)S(1)} %add.92), channel_id=1, source_target_pairs={{0,32},{8,40},{16,48},{24,56},{32,0},{40,8},{48,16},{56,24},{64,96... | collective-permute-start | bytes 245768 | tf_op jit(solution)/shard_map/ppermute | solution.py:463
  43.5 6.6 %collective-permute-start.5 = (f32[32,640]{1,0:T(8,128)S(1)}, f32[32,640]{1,0:T(8,128)S(1)}, u32[]{:S(2)}, u32[]{:S(2)}) collective-permute-start(f32[32,640]{1,0:T(8,128)S(1)} %add.92), channel_id=1, source_target_pairs={{0,16},{8,24},{16,32},{24,40},{32,48},{40,56},{48,0},{56,8},{64,80... | collective-permute-start | bytes 245768 | tf_op jit(solution)/shard_map/ppermute | solution.py:463
  50.2 6.3 %collective-permute-start.10 = (f32[32,640]{1,0:T(8,128)S(1)}, f32[32,640]{1,0:T(8,128)S(1)}, u32[]{:S(2)}, u32[]{:S(2)}) collective-permute-start(f32[32,640]{1,0:T(8,128)S(1)} %add_add_fusion.1), channel_id=1, source_target_pairs={{0,192},{8,200},{16,208},{24,216},{32,224},{40,232},{48,240},{56,2... | collective-permute-start | bytes 245768 | tf_op jit(solution)/shard_map/ppermute | solution.py:463
  53.3 6.0 %collective-permute-start.9 = (f32[32,640]{1,0:T(8,128)S(1)}, f32[32,640]{1,0:T(8,128)S(1)}, u32[]{:S(2)}, u32[]{:S(2)}) collective-permute-start(f32[32,640]{1,0:T(8,128)S(1)} %add_add_fusion.1), channel_id=1, source_target_pairs={{0,128},{8,136},{16,144},{24,152},{32,160},{40,168},{48,176},{56,1... | collective-permute-start | bytes 245768 | tf_op jit(solution)/shard_map/ppermute | solution.py:463
  53.9 6.3 %collective-permute-start.8 = (f32[32,640]{1,0:T(8,128)S(1)}, f32[32,640]{1,0:T(8,128)S(1)}, u32[]{:S(2)}, u32[]{:S(2)}) collective-permute-start(f32[32,640]{1,0:T(8,128)S(1)} %add_add_fusion.1), channel_id=1, source_target_pairs={{0,64},{8,72},{16,80},{24,88},{32,96},{40,104},{48,112},{56,120},{... | collective-permute-start | bytes 245768 | tf_op jit(solution)/shard_map/ppermute | solution.py:463
  60.2 5.9 %collective-permute-start.13 = (f32[32,640]{1,0:T(8,128)S(1)}, f32[32,640]{1,0:T(8,128)S(1)}, u32[]{:S(2)}, u32[]{:S(2)}) collective-permute-start(f32[32,640]{1,0:T(8,128)S(1)} %add_add_fusion), channel_id=1, source_target_pairs={{0,1},{1,2},{2,3},{3,4},{4,5},{5,6},{6,7},{7,0},{8,9},{9,10},{10,1... | collective-permute-start | bytes 245768 | tf_op jit(solution)/shard_map/ppermute | solution.py:459
  60.5 6.2 %collective-permute-start.12 = (f32[32,640]{1,0:T(8,128)S(1)}, f32[32,640]{1,0:T(8,128)S(1)}, u32[]{:S(2)}, u32[]{:S(2)}) collective-permute-start(f32[32,640]{1,0:T(8,128)S(1)} %add_add_fusion), channel_id=1, source_target_pairs={{0,6},{1,7},{2,0},{3,1},{4,2},{5,3},{6,4},{7,5},{8,14},{9,15},{10,... | collective-permute-start | bytes 245768 | tf_op jit(solution)/shard_map/ppermute | solution.py:459
  60.6 7.9 %collective-permute-start.11 = (f32[32,640]{1,0:T(8,128)S(1)}, f32[32,640]{1,0:T(8,128)S(1)}, u32[]{:S(2)}, u32[]{:S(2)}) collective-permute-start(f32[32,640]{1,0:T(8,128)S(1)} %add_add_fusion), channel_id=1, source_target_pairs={{0,7},{1,0},{2,1},{3,2},{4,3},{5,4},{6,5},{7,6},{8,15},{9,8},{10,9... | collective-permute-start | bytes 245768 | tf_op jit(solution)/shard_map/ppermute | solution.py:459
  68.5 9.8 %collective-permute-start.14 = (f32[4,32,640]{2,1,0:T(8,128)S(1)}, f32[4,32,640]{2,1,0:T(8,128)S(1)}, u32[]{:S(2)}, u32[]{:S(2)}) collective-permute-start(f32[4,32,640]{2,1,0:T(8,128)S(1)} %pad_maximum_fusion.mine_ref), channel_id=1, source_target_pairs={{0,8},{8,0},{16,24},{24,16},{32,40},{40,32},{48,56},{56,48},{64,72... | collective-permute-start | bytes 983048 | tf_op jit(solution)/shard_map/ppermute | solution.py:463
  74.7 16.9 %collective-permute-start.18 = (f32[4,72,512]{2,1,0:T(8,128)S(1)}, f32[4,72,512]{2,1,0:T(8,128)S(1)}, u32[]{:S(2)}, u32[]{:S(2)}) collective-permute-start(f32[4,72,512]{2,1,0:T(8,128)S(1)} %get-tuple-element.47), channel_id=1, source_target_pairs={{0,64},{8,72},{16,80},{24,88},{32,96},{40,104},{48,112},{56,120},{... | collective-permute-start | bytes 1769480 | tf_op jit(solution)/shard_map/ppermute | solution.py:463
  74.8 16.8 %collective-permute-start.17 = (f32[4,72,512]{2,1,0:T(8,128)S(1)}, f32[4,72,512]{2,1,0:T(8,128)S(1)}, u32[]{:S(2)}, u32[]{:S(2)}) collective-permute-start(f32[4,72,512]{2,1,0:T(8,128)S(1)} %get-tuple-element.48), channel_id=1, source_target_pairs={{0,16},{8,24},{16,0},{24,8},{32,48},{40,56},{48,32},{56,40},{64,80... | collective-permute-start | bytes 1769480 | tf_op jit(solution)/shard_map/ppermute | solution.py:463
  74.9 29.4 %collective-permute-start.16 = (f32[4,72,512]{2,1,0:T(8,128)S(1)}, f32[4,72,512]{2,1,0:T(8,128)S(1)}, u32[]{:S(2)}, u32[]{:S(2)}) collective-permute-start(f32[4,72,512]{2,1,0:T(8,128)S(1)} %get-tuple-element.49), channel_id=1, source_target_pairs={{0,80},{8,88},{16,64},{24,72},{32,112},{40,120},{48,96},{56,104},{... | collective-permute-start | bytes 1769480 | tf_op jit(solution)/shard_map/ppermute | solution.py:463
  104.5 18.2 %collective-permute-start.21 = (f32[1,72,512]{2,1,0:T(8,128)S(1)}, f32[1,72,512]{2,1,0:T(8,128)S(1)}, u32[]{:S(2)}, u32[]{:S(2)}) collective-permute-start(f32[1,72,512]{2,1,0:T(8,128)S(1)} %get-tuple-element.50), channel_id=1, source_target_pairs={{0,192},{8,200},{16,208},{24,216},{32,224},{40,232},{48,240},{56,2... | collective-permute-start | bytes 442376 | tf_op jit(solution)/shard_map/ppermute | solution.py:463
  105.2 17.6 %collective-permute-start.20 = (f32[1,72,512]{2,1,0:T(8,128)S(1)}, f32[1,72,512]{2,1,0:T(8,128)S(1)}, u32[]{:S(2)}, u32[]{:S(2)}) collective-permute-start(f32[1,72,512]{2,1,0:T(8,128)S(1)} %get-tuple-element.51), channel_id=1, source_target_pairs={{0,48},{8,56},{16,32},{24,40},{32,16},{40,24},{48,0},{56,8},{64,11... | collective-permute-start | bytes 442376 | tf_op jit(solution)/shard_map/ppermute | solution.py:463
  105.7 17.1 %collective-permute-start.19 = (f32[1,72,512]{2,1,0:T(8,128)S(1)}, f32[1,72,512]{2,1,0:T(8,128)S(1)}, u32[]{:S(2)}, u32[]{:S(2)}) collective-permute-start(f32[1,72,512]{2,1,0:T(8,128)S(1)} %get-tuple-element.52), channel_id=1, source_target_pairs={{0,240},{8,248},{16,224},{24,232},{32,208},{40,216},{48,192},{56,2... | collective-permute-start | bytes 442376 | tf_op jit(solution)/shard_map/ppermute | solution.py:463

commit v3 on v2

--- a/solution.py
+++ b/solution.py
@@ -406,8 +406,9 @@
     det_ref[...] = log_refs[0][...] + log_refs[1][...] + log_refs[2][...]
     i2, offset = scales(log_ref, length_ref)
     over = 1.0 / noise_ref[...]
-    rows = own_ref.shape[0]
-    left = widen(own_ref[...], half_norm(own_ref[...]) + offset, True)
+    rows = own_ref.shape[0] // SHARDS
+    own = own_ref[pl.ds(pl.multiple_of(ids_ref[32] * rows, rows), rows), :]
+    left = widen(own, half_norm(own) + offset, True)
     right = widen(panel_ref[...], half_norm(panel_ref[...]), False)
     kern = jnp.exp2(i2 * lax.dot_general(left, right, NT, preferred_element_type=F32))
     row = ids_ref[34] + lax.broadcasted_iota(jnp.int32, (rows, PB), 0)
@@ -428,7 +429,7 @@
 
 def finish(ids, log_scale, lengthscale, noise_var, inducing, panel, *others):
     rows = inducing.shape[0] // SHARDS
-    full = lambda a: pl.BlockSpec(a.shape, lambda i, d: (0,) * a.ndim)
+    full = pl.BlockSpec(memory_space=pltpu.VMEM)
     return pl.pallas_call(
         finish_kernel,
         out_shape=(
@@ -437,18 +438,8 @@
             jax.ShapeDtypeStruct((1, PB), F32),
             jax.ShapeDtypeStruct((1, 1), F32),
         ),
-        grid_spec=pltpu.PrefetchScalarGridSpec(
-            num_scalar_prefetch=1,
-            grid=(1,),
-            in_specs=[single()] * 3 + [pl.BlockSpec((rows, 128), lambda i, d: (d[32], 0))]
-            + [full(a) for a in (panel,) + others],
-            out_specs=(
-                pl.BlockSpec((rows, PB), lambda i, d: (0, 0)),
-                pl.BlockSpec((1, rows), lambda i, d: (0, 0)),
-                pl.BlockSpec((1, PB), lambda i, d: (0, 0)),
-                single(),
-            ),
-        ),
+        in_specs=[pl.BlockSpec(memory_space=pltpu.SMEM)] + [full] * (5 + len(others)),
+        out_specs=(full,) * 4,
         compiler_params=vmem(20 << 20),
         cost_estimate=pl.CostEstimate(flops=10**9, bytes_accessed=2 << 20, transcendentals=1 << 16),
         name="finish",

time: 129 us -> 129 us (level)
  no operation moved by 1% of the time
where the time goes in v3:
time: 129 us; the launch traced here: 127 us
  Pallas kernels  59.1 us (46%)
  starting transfers between devices  33.8 us (26%)
  waiting for transfers between devices  27.9 us (22%)
  between operations  2.88 us (2%)
  local copies, waits for them, and re-layouts  2.14 us (2%)
  other arithmetic  1.48 us (1%)
    ppermute x15, waiting for transfers between devices, across(): return lax.ppermute(x, 'dp', [(i, to(i)) for i in range(SHARDS)])  23.8 us
    ppermute x15, starting transfers between devices, across(): return lax.ppermute(x, 'dp', [(i, to(i)) for i in range(SHARDS)])  19.5 us
    ppermute x7, starting transfers between devices, moved(): return lax.ppermute(x, axis, pairs)  14.3 us
    pallas_call x2, Pallas kernels, embed(): pl.pallas_call(functools.partial(embed_kernel, base), out_shape=jax.Shape...  14.2 us
    pallas_call x1, Pallas kernels, factor_last(): pl.pallas_call(factor_last_kernel, out_shape=(jax.ShapeDtypeStruct(work.s...  12.2 us
    pallas_call x2, Pallas kernels, gram(): pl.pallas_call(gram_kernel, out_shape=jax.ShapeDtypeStruct((count, 72, PB...  11 us
    pallas_call x1, Pallas kernels, factor_first(): pl.pallas_call(factor_first_kernel, out_shape=(jax.ShapeDtypeStruct((128,...  7.47 us
    pallas_call x1, Pallas kernels, factor_middle(): pl.pallas_call(factor_middle_kernel, out_shape=(jax.ShapeDtypeStruct((128...  5.83 us
  transfers between devices with their start and end apart: 22, of which 10 were waited for; matrix products, arithmetic and copies ran while one was open for 1% of the time, Pallas kernels for 40%

profile of v3, /device:TPU:0, one launch (start us, length us, event | category | flops | bytes accessed | tf_op | source)
XLA Modules:
  0.0 127.3 jit_solution(11023080180792264961)
XLA Ops:
  0.6 0.9 slice.75
  1.5 6.9 %collective-permute-start.1 = (bf16[512,128]{1,0:T(8,128)(2,1)S(1)}, bf16[512,128]{1,0:T(8,128)(2,1)S(1)}, u32[]{:S(2)}, u32[]{:S(2)}) collective-permute-start(bf16[512,128]{1,0:T(8,128)(2,1)S(1)} %slice.75), channel_id=1, source_target_pairs={{0,5},{8,13},{16,21},{24,29},{32,37},{40,45},{48,53},{56,61},{64,6... | collective-permute-start | bytes 393224 | tf_op jit(solution)/shard_map/ppermute | solution.py:450
  8.5 1.3 %collective-permute-start = (bf16[512,128]{1,0:T(8,128)(2,1)S(1)}, bf16[512,128]{1,0:T(8,128)(2,1)S(1)}, u32[]{:S(2)}, u32[]{:S(2)}) collective-permute-start(bf16[512,128]{1,0:T(8,128)(2,1)S(1)} %slice.75), channel_id=1, source_target_pairs={{0,3},{8,11},{16,19},{24,27},{32,35},{40,43},{48,51},{56,59},{64,6... | collective-permute-start | bytes 393224 | tf_op jit(solution)/shard_map/ppermute | solution.py:450
  9.9 0.5 compare_select_fusion.2.ids_ref
  10.4 0.0 copy-start.3
  10.4 0.0 copy-start
  10.4 7.1 %embed.2.rest_0_ = bf16[2048,256]{1,0:T(8,128)(2,1)} custom-call(s32[40]{0:T(128)} %compare_select_fusion.2.ids_ref, s32[32]{0:T(128)} %counts_ref.3, bf16[2048,256]{1,0:T(8,128)(2,1)} %x_ref.2, bf16[256,1024]{1,0:T(8,128)(2,1)} %w1_ref.3, bf16[1024,1024]{1,0:T(8,128)(2,1)} %w2_ref.3, bf16[1024,128]{1,0:T(8,128)(2,1)} %w3_ref.3, f32[1,128]{1,0:T(1,128)} %bitcast.39), custom_call_target="tpu_custom_call" | custom-call | flops 3000000000 | bytes 4194304 | tf_op jit(solution)/shard_map/embed/pallas_call | solution.py:79
  18.8 0.0 copy-done.3
  18.8 0.0 collective-permute-done.1
  18.8 0.0 collective-permute-done
  18.8 0.0 copy-done
  18.9 1.3 %collective-permute-start.3 = (bf16[512,128]{1,0:T(8,128)(2,1)S(1)}, bf16[512,128]{1,0:T(8,128)(2,1)S(1)}, u32[]{:S(2)}, u32[]{:S(2)}) collective-permute-start(bf16[512,128]{1,0:T(8,128)(2,1)S(1)} %select_select_fusion.1), channel_id=1, source_target_pairs={{0,7},{3,2},{8,15},{11,10},{16,23},{19,18},{24,31},{27,26},{32,39}... | collective-permute-start | bytes 393224 | tf_op jit(solution)/shard_map/ppermute | solution.py:450
  20.2 1.3 %collective-permute-start.2 = (bf16[512,128]{1,0:T(8,128)(2,1)S(1)}, bf16[512,128]{1,0:T(8,128)(2,1)S(1)}, u32[]{:S(2)}, u32[]{:S(2)}) collective-permute-start(bf16[512,128]{1,0:T(8,128)(2,1)S(1)} %select_select_fusion.1), channel_id=1, source_target_pairs={{0,1},{3,4},{5,6},{8,9},{11,12},{13,14},{16,17},{19,20},{21,22},{2... | collective-permute-start | bytes 393224 | tf_op jit(solution)/shard_map/ppermute | solution.py:450
  21.5 7.1 %embed.3.samples_ref.refs_4_ = bf16[2048,256]{1,0:T(8,128)(2,1)} custom-call(s32[40]{0:T(128)} %compare_select_fusion.2.ids_ref, s32[32]{0:T(128)} %counts_ref.3, bf16[2048,256]{1,0:T(8,128)(2,1)} %x_ref.2, bf16[256,1024]{1,0:T(8,128)(2,1)} %w1_ref.3, bf16[1024,1024]{1,0:T(8,128)(2,1)} %w2_ref.3, ...), custom_call_target="tpu_custom_call", output_to_operand_aliasing={{}: (7, {})} | custom-call | flops 3000000000 | bytes 4194304 | tf_op jit(solution)/shard_map/embed/pallas_call | solution.py:79
  28.6 0.0 collective-permute-done.3
  28.6 0.0 collective-permute-done.2
  28.6 0.0 copy-done.1
  28.6 0.0 copy-start.2
  28.7 1.2 copy-done.2
  29.9 3.9 %panel.1 = (bf16[2048,512]{1,0:T(8,128)(2,1)S(1)}, f32[32,640]{1,0:T(8,128)S(1)}, f32[32,640]{1,0:T(8,128)S(1)}) custom-call(s32[40]{0:T(128)S(1)} %copy-done.1, f32[1,1]{1,0:T(1,128)} %bitcast.17.log_ref, f32[1,1]{1,0:T(1,128)} %bitcast.22.length_ref, bf16[2048,256]{1,0:T(8,128)(2,1)S(1)} %copy-done.2, bf16[512,128]{1,0:T(8,128)(2,1)S(1)} %select_select_fusion.panel_ref, ...), custom_call_target="tpu_custom_call" | custom-call | flops 1500000000 | bytes 4194304 | tf_op jit(solution)/shard_map/panel/pallas_call | solution.py:161
  33.8 0.1 collective-permute-start.4
  33.9 5.5 %gram.2 = f32[16,72,512]{2,1,0:T(8,128)S(1)} custom-call(s32[40]{0:T(128)S(1)} %copy-done.1, f32[1,1]{1,0:T(1,128)} %bitcast.18.log_ref, f32[1,1]{1,0:T(1,128)} %bitcast.23.length_ref, bf16[2048,128]{1,0:T(8,128)(2,1)S(1)} %copy-done, bf16[2048,128]{1,0:T(8,128)(2,1)S(1)} %copy-done, bf16[2048,128]{1,0:T(8,128)(2,1)S(1)} %copy-done, ...), custom_call_target="tpu_custom_call" | custom-call | flops 3200000000 | bytes 6291456 | tf_op jit(solution)/shard_map/gram/pallas_call | solution.py:210
  39.4 0.0 collective-permute-done.4
  39.4 0.6 collective-permute-start.15
  40.0 2.8 %collective-permute-start.7 = (f32[32,640]{1,0:T(8,128)S(1)}, f32[32,640]{1,0:T(8,128)S(1)}, u32[]{:S(2)}, u32[]{:S(2)}) collective-permute-start(f32[32,640]{1,0:T(8,128)S(1)} %add.92), channel_id=1, source_target_pairs={{0,48},{8,56},{16,0},{24,8},{32,16},{40,24},{48,32},{56,40},{64,11... | collective-permute-start | bytes 245768 | tf_op jit(solution)/shard_map/ppermute | solution.py:454
  42.7 0.8 collective-permute-start.6
  43.5 0.9 collective-permute-start.5
  44.4 2.0 %collective-permute-done.7 = f32[32,640]{1,0:T(8,128)S(1)} collective-permute-done((f32[32,640]{1,0:T(8,128)S(1)}, f32[32,640]{1,0:T(8,128)S(1)}, u32[]{:S(2)}, u32[]{:S(2)}) %collective-permute-start.7) | collective-permute-done | bytes 81952 | tf_op jit(solution)/shard_map/ppermute | solution.py:454
  46.5 2.8 %collective-permute-done.6 = f32[32,640]{1,0:T(8,128)S(1)} collective-permute-done((f32[32,640]{1,0:T(8,128)S(1)}, f32[32,640]{1,0:T(8,128)S(1)}, u32[]{:S(2)}, u32[]{:S(2)}) %collective-permute-start.6) | collective-permute-done | bytes 81952 | tf_op jit(solution)/shard_map/ppermute | solution.py:454
  49.3 0.9 collective-permute-done.5
  50.2 3.1 %collective-permute-start.10 = (f32[32,640]{1,0:T(8,128)S(1)}, f32[32,640]{1,0:T(8,128)S(1)}, u32[]{:S(2)}, u32[]{:S(2)}) collective-permute-start(f32[32,640]{1,0:T(8,128)S(1)} %add_add_fusion.1), channel_id=1, source_target_pairs={{0,192},{8,200},{16,208},{24,216},{32,224},{40,232},{48,240},{56,2... | collective-permute-start | bytes 245768 | tf_op jit(solution)/shard_map/ppermute | solution.py:454
  53.3 0.6 collective-permute-start.9
  53.9 1.0 collective-permute-start.8
  54.9 1.6 %collective-permute-done.10 = f32[32,640]{1,0:T(8,128)S(1)} collective-permute-done((f32[32,640]{1,0:T(8,128)S(1)}, f32[32,640]{1,0:T(8,128)S(1)}, u32[]{:S(2)}, u32[]{:S(2)}) %collective-permute-start.10) | collective-permute-done | bytes 81952 | tf_op jit(solution)/shard_map/ppermute | solution.py:454
  56.5 2.8 %collective-permute-done.9 = f32[32,640]{1,0:T(8,128)S(1)} collective-permute-done((f32[32,640]{1,0:T(8,128)S(1)}, f32[32,640]{1,0:T(8,128)S(1)}, u32[]{:S(2)}, u32[]{:S(2)}) %collective-permute-start.9) | collective-permute-done | bytes 81952 | tf_op jit(solution)/shard_map/ppermute | solution.py:454
  59.3 0.9 collective-permute-done.8
  60.2 0.3 collective-permute-start.13
  60.5 0.1 collective-permute-start.12
  60.6 3.1 %collective-permute-start.11 = (f32[32,640]{1,0:T(8,128)S(1)}, f32[32,640]{1,0:T(8,128)S(1)}, u32[]{:S(2)}, u32[]{:S(2)}) collective-permute-start(f32[32,640]{1,0:T(8,128)S(1)} %add_add_fusion), channel_id=1, source_target_pairs={{0,7},{1,0},{2,1},{3,2},{4,3},{5,4},{6,5},{7,6},{8,15},{9,8},{10,9... | collective-permute-start | bytes 245768 | tf_op jit(solution)/shard_map/ppermute | solution.py:450
  64.3 1.8 %collective-permute-done.13 = f32[32,640]{1,0:T(8,128)S(1)} collective-permute-done((f32[32,640]{1,0:T(8,128)S(1)}, f32[32,640]{1,0:T(8,128)S(1)}, u32[]{:S(2)}, u32[]{:S(2)}) %collective-permute-start.13) | collective-permute-done | bytes 81952 | tf_op jit(solution)/shard_map/ppermute | solution.py:450
  66.1 0.6 collective-permute-done.12
  66.7 1.7 %collective-permute-done.11 = f32[32,640]{1,0:T(8,128)S(1)} collective-permute-done((f32[32,640]{1,0:T(8,128)S(1)}, f32[32,640]{1,0:T(8,128)S(1)}, u32[]{:S(2)}, u32[]{:S(2)}) %collective-permute-start.11) | collective-permute-done | bytes 81952 | tf_op jit(solution)/shard_map/ppermute | solution.py:450
  68.5 0.1 collective-permute-start.14
  68.6 5.5 %gram.3 = f32[16,72,512]{2,1,0:T(8,128)S(1)} custom-call(s32[40]{0:T(128)S(1)} %copy-done.1, f32[1,1]{1,0:T(1,128)} %bitcast.20.log_ref, f32[1,1]{1,0:T(1,128)} %bitcast.25.length_ref, bf16[2048,128]{1,0:T(8,128)(2,1)S(1)} %copy-done, bf16[2048,128]{1,0:T(8,128)(2,1)S(1)} %copy-done, bf16[2048,128]{1,0:T(8,128)(2,1)S(1)} %copy-done, ...), custom_call_target="tpu_custom_call" | custom-call | flops 3200000000 | bytes 6291456 | tf_op jit(solution)/shard_map/gram/pallas_call | solution.py:210
  74.1 0.0 collective-permute-done.15
  74.1 0.6 slice_add_fusion.3
  74.7 0.1 collective-permute-start.18
  74.8 0.1 collective-permute-start.17
  74.9 3.4 %collective-permute-start.16 = (f32[4,72,512]{2,1,0:T(8,128)S(1)}, f32[4,72,512]{2,1,0:T(8,128)S(1)}, u32[]{:S(2)}, u32[]{:S(2)}) collective-permute-start(f32[4,72,512]{2,1,0:T(8,128)S(1)} %get-tuple-element.49), channel_id=1, source_target_pairs={{0,80},{8,88},{16,64},{24,72},{32,112},{40,120},{48,96},{56,104},{... | collective-permute-start | bytes 1769480 | tf_op jit(solution)/shard_map/ppermute | solution.py:454
  78.2 0.0 collective-permute-done.14.other_ref
  78.2 7.5 %factor_first.1 = (f32[128,512]{1,0:T(8,128)S(1)}, f32[1,1]{1,0:T(1,128)}, f32[384,512]{1,0:T(8,128)S(1)}, f32[1,512]{1,0:T(1,128)S(1)}) custom-call(s32[40]{0:T(128)S(1)} %copy-done.1, f32[1,1]{1,0:T(1,128)} %bitcast.19.log_ref_in, f32[1,1]{1,0:T(1,128)} %bitcast.24.length_ref, f32[1,1]{1,0:T(1,128)} %bitcast.27.noise_ref, ...), custom_call_target="tpu_custom_call" | custom-call | flops 6000000000 | bytes 2097152 | tf_op jit(solution)/shard_map/factor_first/pallas_call | solution.py:354
  85.7 5.8 %factor_middle.1 = (f32[128,512]{1,0:T(8,128)S(1)}, f32[1,1]{1,0:T(1,128)}, f32[256,512]{1,0:T(8,128)S(1)}) custom-call(f32[384,512]{1,0:T(8,128)S(1)} %get-tuple-element.33.work_ref), custom_call_target="tpu_custom_call" | custom-call | flops 5000000000 | bytes 2097152 | tf_op jit(solution)/shard_map/factor_middle/pallas_call | solution.py:373
  91.5 0.0 collective-permute-done.18
  91.5 0.0 collective-permute-done.17
  91.5 12.7 %collective-permute-done.16 = f32[4,72,512]{2,1,0:T(8,128)S(1)} collective-permute-done((f32[4,72,512]{2,1,0:T(8,128)S(1)}, f32[4,72,512]{2,1,0:T(8,128)S(1)}, u32[]{:S(2)}, u32[]{:S(2)}) %collective-permute-start.16) | collective-permute-done | bytes 589856 | tf_op jit(solution)/shard_map/ppermute | solution.py:454
  104.3 0.3 slice_add_fusion.4
  104.5 0.6 collective-permute-start.21
  105.2 0.5 collective-permute-start.20
  105.7 4.9 %collective-permute-start.19 = (f32[1,72,512]{2,1,0:T(8,128)S(1)}, f32[1,72,512]{2,1,0:T(8,128)S(1)}, u32[]{:S(2)}, u32[]{:S(2)}) collective-permute-start(f32[1,72,512]{2,1,0:T(8,128)S(1)} %get-tuple-element.52), channel_id=1, source_target_pairs={{0,240},{8,248},{16,224},{24,232},{32,208},{40,216},{48,192},{56,2... | collective-permute-start | bytes 442376 | tf_op jit(solution)/shard_map/ppermute | solution.py:454
  110.5 12.2 %factor_last.1 = (f32[256,512]{1,0:T(8,128)S(1)}, f32[1,1]{1,0:T(1,128)}) custom-call(f32[256,512]{1,0:T(8,128)S(1)} %get-tuple-element.35.work_ref), custom_call_target="tpu_custom_call" | custom-call | flops 10000000000 | bytes 2097152 | tf_op jit(solution)/shard_map/factor_last/pallas_call | solution.py:391
  122.8 0.0 collective-permute-done.21
  122.8 0.0 collective-permute-done.20
  122.8 0.0 collective-permute-done.19
  122.8 4.5 %finish.1 = (f32[64,512]{1,0:T(8,128)}, f32[1,64]{1,0:T(1,128)}, f32[1,512]{1,0:T(1,128)}, f32[1,1]{1,0:T(1,128)}) custom-call(s32[40]{0:T(128)S(1)} %copy-done.1, f32[1,1]{1,0:T(1,128)} %bitcast.21.log_ref, f32[1,1]{1,0:T(1,128)} %bitcast.26.length_ref, f32[1,1]{1,0:T(1,128)} %bitcast.28.noise_ref, bf16[2048,128]{1,0:T(8,128)(2,1)S(1)} %copy-done, ...), custom_call_target="tpu_custom_call" | custom-call | flops 1000000000 | bytes 2097152 | tf_op jit(solution)/shard_map/finish/pallas_call | solution.py:433
  (8 shorter events, 0.1 us)
Async XLA Ops:
  1.5 17.3 %collective-permute-start.1 = (bf16[512,128]{1,0:T(8,128)(2,1)S(1)}, bf16[512,128]{1,0:T(8,128)(2,1)S(1)}, u32[]{:S(2)}, u32[]{:S(2)}) collective-permute-start(bf16[512,128]{1,0:T(8,128)(2,1)S(1)} %slice.75), channel_id=1, source_target_pairs={{0,5},{8,13},{16,21},{24,29},{32,37},{40,45},{48,53},{56,61},{64,6... | collective-permute-start | bytes 393224 | tf_op jit(solution)/shard_map/ppermute | solution.py:450
  8.5 10.3 %collective-permute-start = (bf16[512,128]{1,0:T(8,128)(2,1)S(1)}, bf16[512,128]{1,0:T(8,128)(2,1)S(1)}, u32[]{:S(2)}, u32[]{:S(2)}) collective-permute-start(bf16[512,128]{1,0:T(8,128)(2,1)S(1)} %slice.75), channel_id=1, source_target_pairs={{0,3},{8,11},{16,19},{24,27},{32,35},{40,43},{48,51},{56,59},{64,6... | collective-permute-start | bytes 393224 | tf_op jit(solution)/shard_map/ppermute | solution.py:450
  10.4 8.4 %copy-start.3 = (bf16[2048]{0:T(1024)(128)(2,1)S(1)}, bf16[2048]{0:T(1024)(128)(2,1)}, u32[]{:S(2)}) copy-start(bf16[2048]{0:T(1024)(128)(2,1)} %param.12) | copy-start | bytes 12292
  10.4 8.5 %copy-start = (bf16[2048,128]{1,0:T(8,128)(2,1)S(1)}, bf16[2048,128]{1,0:T(8,128)(2,1)}, u32[]{:S(2)}) copy-start(bf16[2048,128]{1,0:T(8,128)(2,1)} %own_ref.1) | copy-start | bytes 1572868
  18.9 9.7 %copy-start.1 = (s32[40]{0:T(128)S(1)}, s32[40]{0:T(128)}, u32[]{:S(2)}) copy-start(s32[40]{0:T(128)} %compare_select_fusion.2.ids_ref) | copy-start | bytes 484
  18.9 9.7 %collective-permute-start.3 = (bf16[512,128]{1,0:T(8,128)(2,1)S(1)}, bf16[512,128]{1,0:T(8,128)(2,1)S(1)}, u32[]{:S(2)}, u32[]{:S(2)}) collective-permute-start(bf16[512,128]{1,0:T(8,128)(2,1)S(1)} %select_select_fusion.1), channel_id=1, source_target_pairs={{0,7},{3,2},{8,15},{11,10},{16,23},{19,18},{24,31},{27,26},{32,39}... | collective-permute-start | bytes 393224 | tf_op jit(solution)/shard_map/ppermute | solution.py:450
  20.2 8.4 %collective-permute-start.2 = (bf16[512,128]{1,0:T(8,128)(2,1)S(1)}, bf16[512,128]{1,0:T(8,128)(2,1)S(1)}, u32[]{:S(2)}, u32[]{:S(2)}) collective-permute-start(bf16[512,128]{1,0:T(8,128)(2,1)S(1)} %select_select_fusion.1), channel_id=1, source_target_pairs={{0,1},{3,4},{5,6},{8,9},{11,12},{13,14},{16,17},{19,20},{21,22},{2... | collective-permute-start | bytes 393224 | tf_op jit(solution)/shard_map/ppermute | solution.py:450
  28.6 1.2 copy-start.2
  33.8 5.6 %collective-permute-start.4 = (f32[32,640]{1,0:T(8,128)S(1)}, f32[32,640]{1,0:T(8,128)S(1)}, u32[]{:S(2)}, u32[]{:S(2)}) collective-permute-start(f32[32,640]{1,0:T(8,128)S(1)} %get-tuple-element.28), channel_id=1, source_target_pairs={{0,8},{8,0},{16,24},{24,16},{32,40},{40,32},{48,56},{56,48},{64,72... | collective-permute-start | bytes 245768 | tf_op jit(solution)/shard_map/ppermute | solution.py:454
  39.4 34.7 %collective-permute-start.15 = (f32[16,72,512]{2,1,0:T(8,128)S(1)}, f32[16,72,512]{2,1,0:T(8,128)S(1)}, u32[]{:S(2)}, u32[]{:S(2)}) collective-permute-start(f32[16,72,512]{2,1,0:T(8,128)S(1)} %gram.2), channel_id=1, source_target_pairs={{0,8},{8,0},{16,24},{24,16},{32,40},{40,32},{48,56},{56,48},{64,72... | collective-permute-start | bytes 7077896 | tf_op jit(solution)/shard_map/ppermute | solution.py:454
  40.0 6.5 %collective-permute-start.7 = (f32[32,640]{1,0:T(8,128)S(1)}, f32[32,640]{1,0:T(8,128)S(1)}, u32[]{:S(2)}, u32[]{:S(2)}) collective-permute-start(f32[32,640]{1,0:T(8,128)S(1)} %add.92), channel_id=1, source_target_pairs={{0,48},{8,56},{16,0},{24,8},{32,16},{40,24},{48,32},{56,40},{64,11... | collective-permute-start | bytes 245768 | tf_op jit(solution)/shard_map/ppermute | solution.py:454
  42.7 6.5 %collective-permute-start.6 = (f32[32,640]{1,0:T(8,128)S(1)}, f32[32,640]{1,0:T(8,128)S(1)}, u32[]{:S(2)}, u32[]{:S(2)}) collective-permute-start(f32[32,640]{1,0:T(8,128)S(1)} %add.92), channel_id=1, source_target_pairs={{0,32},{8,40},{16,48},{24,56},{32,0},{40,8},{48,16},{56,24},{64,96... | collective-permute-start | bytes 245768 | tf_op jit(solution)/shard_map/ppermute | solution.py:454
  43.5 6.6 %collective-permute-start.5 = (f32[32,640]{1,0:T(8,128)S(1)}, f32[32,640]{1,0:T(8,128)S(1)}, u32[]{:S(2)}, u32[]{:S(2)}) collective-permute-start(f32[32,640]{1,0:T(8,128)S(1)} %add.92), channel_id=1, source_target_pairs={{0,16},{8,24},{16,32},{24,40},{32,48},{40,56},{48,0},{56,8},{64,80... | collective-permute-start | bytes 245768 | tf_op jit(solution)/shard_map/ppermute | solution.py:454
  50.2 6.3 %collective-permute-start.10 = (f32[32,640]{1,0:T(8,128)S(1)}, f32[32,640]{1,0:T(8,128)S(1)}, u32[]{:S(2)}, u32[]{:S(2)}) collective-permute-start(f32[32,640]{1,0:T(8,128)S(1)} %add_add_fusion.1), channel_id=1, source_target_pairs={{0,192},{8,200},{16,208},{24,216},{32,224},{40,232},{48,240},{56,2... | collective-permute-start | bytes 245768 | tf_op jit(solution)/shard_map/ppermute | solution.py:454
  53.3 6.0 %collective-permute-start.9 = (f32[32,640]{1,0:T(8,128)S(1)}, f32[32,640]{1,0:T(8,128)S(1)}, u32[]{:S(2)}, u32[]{:S(2)}) collective-permute-start(f32[32,640]{1,0:T(8,128)S(1)} %add_add_fusion.1), channel_id=1, source_target_pairs={{0,128},{8,136},{16,144},{24,152},{32,160},{40,168},{48,176},{56,1... | collective-permute-start | bytes 245768 | tf_op jit(solution)/shard_map/ppermute | solution.py:454
  53.9 6.3 %collective-permute-start.8 = (f32[32,640]{1,0:T(8,128)S(1)}, f32[32,640]{1,0:T(8,128)S(1)}, u32[]{:S(2)}, u32[]{:S(2)}) collective-permute-start(f32[32,640]{1,0:T(8,128)S(1)} %add_add_fusion.1), channel_id=1, source_target_pairs={{0,64},{8,72},{16,80},{24,88},{32,96},{40,104},{48,112},{56,120},{... | collective-permute-start | bytes 245768 | tf_op jit(solution)/shard_map/ppermute | solution.py:454
  60.2 5.9 %collective-permute-start.13 = (f32[32,640]{1,0:T(8,128)S(1)}, f32[32,640]{1,0:T(8,128)S(1)}, u32[]{:S(2)}, u32[]{:S(2)}) collective-permute-start(f32[32,640]{1,0:T(8,128)S(1)} %add_add_fusion), channel_id=1, source_target_pairs={{0,1},{1,2},{2,3},{3,4},{4,5},{5,6},{6,7},{7,0},{8,9},{9,10},{10,1... | collective-permute-start | bytes 245768 | tf_op jit(solution)/shard_map/ppermute | solution.py:450
  60.5 6.2 %collective-permute-start.12 = (f32[32,640]{1,0:T(8,128)S(1)}, f32[32,640]{1,0:T(8,128)S(1)}, u32[]{:S(2)}, u32[]{:S(2)}) collective-permute-start(f32[32,640]{1,0:T(8,128)S(1)} %add_add_fusion), channel_id=1, source_target_pairs={{0,6},{1,7},{2,0},{3,1},{4,2},{5,3},{6,4},{7,5},{8,14},{9,15},{10,... | collective-permute-start | bytes 245768 | tf_op jit(solution)/shard_map/ppermute | solution.py:450
  60.6 7.9 %collective-permute-start.11 = (f32[32,640]{1,0:T(8,128)S(1)}, f32[32,640]{1,0:T(8,128)S(1)}, u32[]{:S(2)}, u32[]{:S(2)}) collective-permute-start(f32[32,640]{1,0:T(8,128)S(1)} %add_add_fusion), channel_id=1, source_target_pairs={{0,7},{1,0},{2,1},{3,2},{4,3},{5,4},{6,5},{7,6},{8,15},{9,8},{10,9... | collective-permute-start | bytes 245768 | tf_op jit(solution)/shard_map/ppermute | solution.py:450
  68.5 9.8 %collective-permute-start.14 = (f32[4,32,640]{2,1,0:T(8,128)S(1)}, f32[4,32,640]{2,1,0:T(8,128)S(1)}, u32[]{:S(2)}, u32[]{:S(2)}) collective-permute-start(f32[4,32,640]{2,1,0:T(8,128)S(1)} %pad_maximum_fusion.mine_ref), channel_id=1, source_target_pairs={{0,8},{8,0},{16,24},{24,16},{32,40},{40,32},{48,56},{56,48},{64,72... | collective-permute-start | bytes 983048 | tf_op jit(solution)/shard_map/ppermute | solution.py:454
  74.7 16.9 %collective-permute-start.18 = (f32[4,72,512]{2,1,0:T(8,128)S(1)}, f32[4,72,512]{2,1,0:T(8,128)S(1)}, u32[]{:S(2)}, u32[]{:S(2)}) collective-permute-start(f32[4,72,512]{2,1,0:T(8,128)S(1)} %get-tuple-element.47), channel_id=1, source_target_pairs={{0,64},{8,72},{16,80},{24,88},{32,96},{40,104},{48,112},{56,120},{... | collective-permute-start | bytes 1769480 | tf_op jit(solution)/shard_map/ppermute | solution.py:454
  74.8 16.8 %collective-permute-start.17 = (f32[4,72,512]{2,1,0:T(8,128)S(1)}, f32[4,72,512]{2,1,0:T(8,128)S(1)}, u32[]{:S(2)}, u32[]{:S(2)}) collective-permute-start(f32[4,72,512]{2,1,0:T(8,128)S(1)} %get-tuple-element.48), channel_id=1, source_target_pairs={{0,16},{8,24},{16,0},{24,8},{32,48},{40,56},{48,32},{56,40},{64,80... | collective-permute-start | bytes 1769480 | tf_op jit(solution)/shard_map/ppermute | solution.py:454
  74.9 29.4 %collective-permute-start.16 = (f32[4,72,512]{2,1,0:T(8,128)S(1)}, f32[4,72,512]{2,1,0:T(8,128)S(1)}, u32[]{:S(2)}, u32[]{:S(2)}) collective-permute-start(f32[4,72,512]{2,1,0:T(8,128)S(1)} %get-tuple-element.49), channel_id=1, source_target_pairs={{0,80},{8,88},{16,64},{24,72},{32,112},{40,120},{48,96},{56,104},{... | collective-permute-start | bytes 1769480 | tf_op jit(solution)/shard_map/ppermute | solution.py:454
  104.5 18.2 %collective-permute-start.21 = (f32[1,72,512]{2,1,0:T(8,128)S(1)}, f32[1,72,512]{2,1,0:T(8,128)S(1)}, u32[]{:S(2)}, u32[]{:S(2)}) collective-permute-start(f32[1,72,512]{2,1,0:T(8,128)S(1)} %get-tuple-element.50), channel_id=1, source_target_pairs={{0,192},{8,200},{16,208},{24,216},{32,224},{40,232},{48,240},{56,2... | collective-permute-start | bytes 442376 | tf_op jit(solution)/shard_map/ppermute | solution.py:454
  105.2 17.6 %collective-permute-start.20 = (f32[1,72,512]{2,1,0:T(8,128)S(1)}, f32[1,72,512]{2,1,0:T(8,128)S(1)}, u32[]{:S(2)}, u32[]{:S(2)}) collective-permute-start(f32[1,72,512]{2,1,0:T(8,128)S(1)} %get-tuple-element.51), channel_id=1, source_target_pairs={{0,48},{8,56},{16,32},{24,40},{32,16},{40,24},{48,0},{56,8},{64,11... | collective-permute-start | bytes 442376 | tf_op jit(solution)/shard_map/ppermute | solution.py:454
  105.7 17.1 %collective-permute-start.19 = (f32[1,72,512]{2,1,0:T(8,128)S(1)}, f32[1,72,512]{2,1,0:T(8,128)S(1)}, u32[]{:S(2)}, u32[]{:S(2)}) collective-permute-start(f32[1,72,512]{2,1,0:T(8,128)S(1)} %get-tuple-element.52), channel_id=1, source_target_pairs={{0,240},{8,248},{16,224},{24,232},{32,208},{40,216},{48,192},{56,2... | collective-permute-start | bytes 442376 | tf_op jit(solution)/shard_map/ppermute | solution.py:454
